TPU v7x, 256 devices: a whole 4x4x8 slice. The times are simulated.
256 devices in a mesh: ctx: 64 (over x, y_hi, z), tp: 4 (over y_lo, core).
Axes of the slice: x: 4, y: 4 (y_hi: 2, y_lo: 2; y = y_hi * 2 + y_lo), z: 8, core: 2. Of those that a mesh axis runs over, the one named last changes fastest.
Arguments:
- queries: bfloat16 [16384, 2048], P('ctx', 'tp'), may hold values from -6 to 6
- keys: bfloat16 [16384, 2048], P('ctx', 'tp'), may hold values from -6 to 6
- values: bfloat16 [16384, 2048], P('ctx', 'tp'), may hold values from -6 to 6
- out_grad: bfloat16 [16384, 4096], P('ctx', 'tp'), may hold values from -6 to 6
- w_out: bfloat16 [2048, 4096], P('tp'), may hold values from -0.09375 to 0.09375
- offsets: int32 [16, 3], P('tp'), may hold values from 0 to 3, as said below
Outputs:
- query_grad: bfloat16 [16384, 2048], P('ctx', 'tp')
- key_grad: bfloat16 [16384, 2048], P('ctx', 'tp')
- value_grad: bfloat16 [16384, 2048], P('ctx', 'tp')
Inputs may be any that keep to these rules, and one draw needn't show every extreme that they name: offsets[h, l] lies between 0 and 2^l - 1.
All inputs are finite; a program needn't handle non-finite values.
Results may differ from a plain program's by a relative error of at most 0.017.
Values may be sent and summed in bfloat16 or wider, within the bound.
No kernel may reach another device: no remote copies, remote signals or barrier semaphores. Data moves between devices by JAX's collectives and lax.ppermute only.
A program may use at most 64 MiB of HBM per device.

v0:
```python
from functools import reduce
import math
import jax
import jax.numpy as jnp
from jax import lax
from jax.sharding import PartitionSpec as P

LEVELS = 3
KEYS_SEG = 1024
NEGATIVE_FILL = -1e30


def for_sending(array):

    def short(part):
        return part.astype(jnp.bfloat16) if part.dtype == jnp.float32 else part

    return jax.tree.map(short, array)


def passed_along(block, axis, distance):
    devices = range(lax.axis_size(axis))
    route = [((i - distance) % len(devices), i) for i in devices]
    return lax.ppermute(block, axis, route)


def pick_table(offset_col, stride):
    return lax.broadcasted_iota(jnp.int32, (stride, offset_col.shape[0]), 0) == offset_col[None, :]


def pack_rows(whole, pick):
    stride = pick.shape[0]
    grouped = whole.reshape((whole.shape[0] // stride, stride) + whole.shape[1:])
    chosen = pick.reshape((1,) + pick.shape + (1,) * (whole.ndim - 2))
    return jnp.sum(jnp.where(chosen, grouped, jnp.zeros((), whole.dtype)), axis=1)


def spread_rows(packed, pick, fill_value):
    stride = pick.shape[0]
    chosen = pick.reshape((1,) + pick.shape + (1,) * (packed.ndim - 2))
    spread = jnp.where(chosen, packed[:, None], jnp.asarray(fill_value, packed.dtype))
    return spread.reshape((packed.shape[0] * stride,) + packed.shape[1:])


def linked_pairs(offset_col, stride, segment, query_start, key_start, row_count):
    tok_rows = row_count * stride
    total_rows = tok_rows * lax.axis_size("ctx")
    rotation = 2 * tok_rows
    lanes = lax.broadcasted_iota(jnp.int32, (row_count,), 0) * stride
    query_pos = (
        query_start + lanes[None, :, None] + offset_col[:, None, None] - rotation
    ) % total_rows
    key_pos = (key_start + lanes[None, None, :] + offset_col[:, None, None] - rotation) % total_rows
    return (query_pos // segment == key_pos // segment) & (key_pos <= query_pos)


def forward_tile(running, query_pack, key_pair, linked, score_scale):
    row_top, row_total, accumulated = running
    scores = (
        jnp.einsum("ahd,bhd->hab", query_pack, key_pair[0], preferred_element_type=jnp.float32)
        * score_scale
    )
    scores = jnp.where(linked, scores, NEGATIVE_FILL)
    new_top = jnp.maximum(row_top, jnp.max(scores, axis=2).T)
    weights = jnp.where(linked, jnp.exp(scores - new_top.T[:, :, None]), 0.0)
    factor = jnp.exp(row_top - new_top)
    row_total = row_total * factor + jnp.sum(weights, axis=2).T
    weights_high = weights.astype(jnp.bfloat16)
    weights_rest = (weights - weights_high.astype(jnp.float32)).astype(jnp.bfloat16)
    product = jnp.einsum(
        "hab,bhd->ahd", weights_high, key_pair[1], preferred_element_type=jnp.float32
    )
    product = product + jnp.einsum(
        "hab,bhd->ahd", weights_rest, key_pair[1], preferred_element_type=jnp.float32
    )
    accumulated = accumulated * factor[:, :, None] + product
    return (new_top, row_total, accumulated)


def tile_grads(query_side, key_pair, linked, score_scale):
    query_pack, grad_pack, log_pack, delta_pack = query_side
    scores = (
        jnp.einsum("ahd,bhd->hab", query_pack, key_pair[0], preferred_element_type=jnp.float32)
        * score_scale
    )
    scores = jnp.where(linked, scores, NEGATIVE_FILL)
    weights = jnp.where(linked, jnp.exp(scores - log_pack.T[:, :, None]), 0.0)
    prob_grad = jnp.einsum(
        "ahd,bhd->hab", grad_pack, key_pair[1], preferred_element_type=jnp.float32
    )
    score_grad = (weights * (prob_grad - delta_pack.T[:, :, None])).astype(jnp.bfloat16)
    return (weights.astype(jnp.bfloat16), score_grad)


def forward_relay(
    running, query_pack, key_pair, offset_col, stride, segment, relay_turns, score_scale
):
    row_count = query_pack.shape[0]
    tok_rows = row_count * stride
    axis_size = lax.axis_size("ctx")
    device_index = lax.axis_index("ctx")
    stored = (
        jnp.zeros((max(relay_turns, 1),) + key_pair[0].shape, key_pair[0].dtype),
        jnp.zeros((max(relay_turns, 1),) + key_pair[1].shape, key_pair[1].dtype),
    )

    def forward_turn_body(turn_num, carried):
        packet, running, stored = carried
        packet = jax.tree.map(
            lambda part, own: part.astype(own.dtype),
            passed_along(for_sending(packet), "ctx", 1),
            packet,
        )
        key_start = (device_index - turn_num) % axis_size * tok_rows
        linked = linked_pairs(
            offset_col, stride, segment, device_index * tok_rows, key_start, row_count
        )
        running = forward_tile(running, query_pack, packet, linked, score_scale)
        return (packet, running, stored)

    packet, running, stored = lax.fori_loop(
        1, relay_turns + 1, forward_turn_body, (key_pair, running, stored)
    )
    return (running, stored)


def keys_pass(query_side, key_pair, offset_col, stride, segment, relay_turns, score_scale):
    query_pack, grad_pack = (query_side[0], query_side[1])
    row_count = query_pack.shape[0]
    tok_rows = row_count * stride
    axis_size = lax.axis_size("ctx")
    device_index = lax.axis_index("ctx")
    own_start = device_index * tok_rows
    weights_low, score_grad = tile_grads(
        query_side,
        key_pair,
        linked_pairs(offset_col, stride, segment, own_start, own_start, row_count),
        score_scale,
    )
    level_q = jnp.einsum(
        "hab,bhd->ahd", score_grad, key_pair[0], preferred_element_type=jnp.float32
    )
    partial_value = (
        jnp.einsum("hab,ahd->bhd", score_grad, query_pack, preferred_element_type=jnp.float32),
        jnp.einsum("hab,ahd->bhd", weights_low, grad_pack, preferred_element_type=jnp.float32),
    )

    def keys_turn_body(turn_num, carried):
        packet, partial_value, level_q = carried
        packet = jax.tree.map(
            lambda part, own: part.astype(own.dtype),
            passed_along(for_sending(packet), "ctx", 1),
            packet,
        )
        partial_value = jax.tree.map(
            lambda part, own: part.astype(own.dtype),
            passed_along(for_sending(partial_value), "ctx", 1),
            partial_value,
        )
        key_start = (device_index - turn_num) % axis_size * tok_rows
        weights_low, score_grad = tile_grads(
            query_side,
            packet,
            linked_pairs(offset_col, stride, segment, own_start, key_start, row_count),
            score_scale,
        )
        level_q = level_q + jnp.einsum(
            "hab,bhd->ahd", score_grad, packet[0], preferred_element_type=jnp.float32
        )
        partial_value = (
            partial_value[0]
            + jnp.einsum(
                "hab,ahd->bhd", score_grad, query_pack, preferred_element_type=jnp.float32
            ),
            partial_value[1]
            + jnp.einsum(
                "hab,ahd->bhd", weights_low, grad_pack, preferred_element_type=jnp.float32
            ),
        )
        return (packet, partial_value, level_q)

    packet, partial_value, level_q = lax.fori_loop(
        1, relay_turns + 1, keys_turn_body, (key_pair, partial_value, level_q)
    )
    partial_value = (
        passed_along(partial_value[0].astype(jnp.bfloat16), "ctx", -relay_turns).astype(
            jnp.float32
        ),
        passed_along(partial_value[1].astype(jnp.bfloat16), "ctx", -relay_turns).astype(
            jnp.float32
        ),
    )
    return (level_q, partial_value[0], partial_value[1])


def local(queries, keys, values, out_grad, w_out, offsets):
    tok_rows = queries.shape[0]
    head_count = offsets.shape[0]
    head_width = queries.shape[1] // head_count
    axis_size = lax.axis_size("ctx")
    device_index = lax.axis_index("ctx")
    keys_seg = KEYS_SEG
    score_scale = 1.0 / math.sqrt(head_width)
    own_start = device_index * tok_rows
    query_rows = queries.reshape(tok_rows, head_count, head_width)
    key_rows = keys.reshape(tok_rows, head_count, head_width)
    value_rows = values.reshape(tok_rows, head_count, head_width)
    grad_out = jnp.einsum(
        "td,fd->tf",
        lax.all_gather(out_grad, "tp", axis=1, tiled=True),
        w_out,
        preferred_element_type=jnp.float32,
    )
    grad_rows = grad_out.astype(jnp.bfloat16).reshape(tok_rows, head_count, head_width)
    level_data = []
    for level_num in range(LEVELS):
        stride = 2**level_num
        segment = min(keys_seg * stride, tok_rows * axis_size)
        row_count = tok_rows // stride
        relay_turns = min(max(segment // tok_rows, 1), axis_size) - 1
        offset_col = offsets[:, level_num]
        pick = pick_table(offset_col, stride)
        query_pack = pack_rows(query_rows, pick)
        key_pair = (pack_rows(key_rows, pick), pack_rows(value_rows, pick))
        running = (
            jnp.full((row_count, head_count), NEGATIVE_FILL, jnp.float32),
            jnp.zeros((row_count, head_count), jnp.float32),
            jnp.zeros((row_count, head_count, head_width), jnp.float32),
        )
        linked = linked_pairs(offset_col, stride, segment, own_start, own_start, row_count)
        running = forward_tile(running, query_pack, key_pair, linked, score_scale)
        running, stored = forward_relay(
            running, query_pack, key_pair, offset_col, stride, segment, relay_turns, score_scale
        )
        level_data.append(
            (stride, segment, relay_turns, offset_col, pick, query_pack, key_pair, running, stored)
        )
    tops = [spread_rows(entry[7][0], entry[4], NEGATIVE_FILL) for entry in level_data]
    row_top = reduce(jnp.maximum, tops)
    row_total = jnp.zeros((tok_rows, head_count), jnp.float32)
    out_sum = jnp.zeros((tok_rows, head_count, head_width), jnp.float32)
    for entry, level_top in zip(level_data, tops):
        factor = jnp.exp(level_top - row_top)
        row_total = row_total + spread_rows(entry[7][1], entry[4], 0.0) * factor
        out_sum = out_sum + spread_rows(entry[7][2], entry[4], 0.0) * factor[:, :, None]
    log_total = row_top + jnp.log(row_total)
    attn_out = out_sum / row_total[:, :, None]
    delta_rows = jnp.sum(grad_rows.astype(jnp.float32) * attn_out, axis=2)
    grad_q = jnp.zeros((tok_rows, head_count, head_width), jnp.float32)
    grad_k = jnp.zeros((tok_rows, head_count, head_width), jnp.float32)
    grad_v = jnp.zeros((tok_rows, head_count, head_width), jnp.float32)
    for (
        stride,
        segment,
        relay_turns,
        offset_col,
        pick,
        query_pack,
        key_pair,
        running,
        stored,
    ) in level_data:
        query_side = (
            query_pack,
            pack_rows(grad_rows, pick),
            pack_rows(log_total, pick),
            pack_rows(delta_rows, pick),
        )
        level_q, level_k, level_v = keys_pass(
            query_side, key_pair, offset_col, stride, segment, relay_turns, score_scale
        )
        grad_q = grad_q + spread_rows(level_q, pick, 0.0)
        grad_k = grad_k + spread_rows(level_k, pick, 0.0)
        grad_v = grad_v + spread_rows(level_v, pick, 0.0)
    flat_width = head_count * head_width
    return (
        (grad_q * score_scale).reshape(tok_rows, flat_width).astype(jnp.bfloat16),
        (grad_k * score_scale).reshape(tok_rows, flat_width).astype(jnp.bfloat16),
        grad_v.reshape(tok_rows, flat_width).astype(jnp.bfloat16),
    )


def solution(mesh):
    return jax.shard_map(
        local,
        mesh=mesh,
        in_specs=(
            P("ctx", "tp"),
            P("ctx", "tp"),
            P("ctx", "tp"),
            P("ctx", "tp"),
            P("tp", None),
            P("tp", None),
        ),
        out_specs=(P("ctx", "tp"), P("ctx", "tp"), P("ctx", "tp")),
        check_vma=False,
    )
```

profile of v0, /device:TPU:8, one launch (start us, length us, event | category | flops | bytes accessed | tf_op | source)
XLA Modules:
  0.0 897.6 jit_solution(7576920657588802797)
XLA Ops:
  20.9 21.8 %all-gather.2.cloned.1.call-done = bf16[256,4096]{1,0:T(8,128)(2,1)} async-done(((bf16[256,1024]{1,0:T(8,128)(2,1)}), bf16[256,4096]{1,0:T(8,128)(2,1)}) %all-gather.2.cloned.1.call-update) | async-done | bytes 2097168 | tf_op jit(solution)/shard_map/all_gather | solution.py:210
  69.5 71.6 %while.144 = (s32[]{:T(128)}, bf16[256,4,128]{2,0,1:T(8,128)(2,1)}, bf16[256,4,128]{2,0,1:T(8,128)(2,1)}, f32[256,4]{0,1:T(4,128)S(1)}, f32[256,4]{0,1:T(4,128)S...) while((s32[]{:T(128)}, bf16[256,4,128]{2,0,1:T(8,128)(2,1)}, ...), condition=%wide.region_5.6_spmd, body=%wide.region_2.5_spmd.sunk | while | flops 208857616 | bytes 10641786 | solution.py:121
  74.0 10.9 %collective-permute-done = bf16[256,4,128]{2,0,1:T(8,128)(2,1)S(1)} collective-permute-done((bf16[256,4,128]{2,0,1:T(8,128)(2,1)}, bf16[256,4,128]{2,0,1:T(8,128)(2,1)S(1)}, u32[]{:S(2)}, u32[]{:S(2)}) %collective-permute-start) | collective-permute-done | bytes 262176 | tf_op jit(solution)/shard_map/while/body/eval_jaxpr/ppermute | solution.py:24
  95.3 14.3 %collective-permute-done = bf16[256,4,128]{2,0,1:T(8,128)(2,1)S(1)} collective-permute-done((bf16[256,4,128]{2,0,1:T(8,128)(2,1)}, bf16[256,4,128]{2,0,1:T(8,128)(2,1)S(1)}, u32[]{:S(2)}, u32[]{:S(2)}) %collective-permute-start) | collective-permute-done | bytes 262176 | tf_op jit(solution)/shard_map/while/body/eval_jaxpr/ppermute | solution.py:24
  119.1 14.3 %collective-permute-done = bf16[256,4,128]{2,0,1:T(8,128)(2,1)S(1)} collective-permute-done((bf16[256,4,128]{2,0,1:T(8,128)(2,1)}, bf16[256,4,128]{2,0,1:T(8,128)(2,1)S(1)}, u32[]{:S(2)}, u32[]{:S(2)}) %collective-permute-start) | collective-permute-done | bytes 262176 | tf_op jit(solution)/shard_map/while/body/eval_jaxpr/ppermute | solution.py:24
  141.9 173.4 %while.146 = (s32[]{:T(128)}, bf16[64,4,128]{2,0,1:T(8,128)(2,1)S(1)}, bf16[64,4,128]{2,0,1:T(8,128)(2,1)S(1)}, f32[64,4]{0,1:T(4,128)S(1)}, f32[64,4]{0,1:T(4,1...) while((s32[]{:T(128)}, ...), condition=%wide.region_23.24_spmd, body=%wide.region_20.23_spmd.sunk | while | flops 13138703 | bytes 1874298 | solution.py:121
  211.5 9.4 %collective-permute-done.4 = bf16[64,4,128]{2,0,1:T(8,128)(2,1)S(1)} collective-permute-done((bf16[64,4,128]{2,0,1:T(8,128)(2,1)S(1)}, bf16[64,4,128]{2,0,1:T(8,128)(2,1)S(1)}, u32[]{:S(2)}, u32[]{:S(2)}) %collective-permute-start.4) | collective-permute-done | bytes 65568 | tf_op jit(solution)/shard_map/while/body/eval_jaxpr/ppermute | solution.py:24
  223.9 9.8 %collective-permute-done.4 = bf16[64,4,128]{2,0,1:T(8,128)(2,1)S(1)} collective-permute-done((bf16[64,4,128]{2,0,1:T(8,128)(2,1)S(1)}, bf16[64,4,128]{2,0,1:T(8,128)(2,1)S(1)}, u32[]{:S(2)}, u32[]{:S(2)}) %collective-permute-start.4) | collective-permute-done | bytes 65568 | tf_op jit(solution)/shard_map/while/body/eval_jaxpr/ppermute | solution.py:24
  236.1 9.1 %collective-permute-done.4 = bf16[64,4,128]{2,0,1:T(8,128)(2,1)S(1)} collective-permute-done((bf16[64,4,128]{2,0,1:T(8,128)(2,1)S(1)}, bf16[64,4,128]{2,0,1:T(8,128)(2,1)S(1)}, u32[]{:S(2)}, u32[]{:S(2)}) %collective-permute-start.4) | collective-permute-done | bytes 65568 | tf_op jit(solution)/shard_map/while/body/eval_jaxpr/ppermute | solution.py:24
  247.5 9.1 %collective-permute-done.4 = bf16[64,4,128]{2,0,1:T(8,128)(2,1)S(1)} collective-permute-done((bf16[64,4,128]{2,0,1:T(8,128)(2,1)S(1)}, bf16[64,4,128]{2,0,1:T(8,128)(2,1)S(1)}, u32[]{:S(2)}, u32[]{:S(2)}) %collective-permute-start.4) | collective-permute-done | bytes 65568 | tf_op jit(solution)/shard_map/while/body/eval_jaxpr/ppermute | solution.py:24
  259.0 9.1 %collective-permute-done.4 = bf16[64,4,128]{2,0,1:T(8,128)(2,1)S(1)} collective-permute-done((bf16[64,4,128]{2,0,1:T(8,128)(2,1)S(1)}, bf16[64,4,128]{2,0,1:T(8,128)(2,1)S(1)}, u32[]{:S(2)}, u32[]{:S(2)}) %collective-permute-start.4) | collective-permute-done | bytes 65568 | tf_op jit(solution)/shard_map/while/body/eval_jaxpr/ppermute | solution.py:24
  270.4 9.1 %collective-permute-done.4 = bf16[64,4,128]{2,0,1:T(8,128)(2,1)S(1)} collective-permute-done((bf16[64,4,128]{2,0,1:T(8,128)(2,1)S(1)}, bf16[64,4,128]{2,0,1:T(8,128)(2,1)S(1)}, u32[]{:S(2)}, u32[]{:S(2)}) %collective-permute-start.4) | collective-permute-done | bytes 65568 | tf_op jit(solution)/shard_map/while/body/eval_jaxpr/ppermute | solution.py:24
  281.9 9.1 %collective-permute-done.4 = bf16[64,4,128]{2,0,1:T(8,128)(2,1)S(1)} collective-permute-done((bf16[64,4,128]{2,0,1:T(8,128)(2,1)S(1)}, bf16[64,4,128]{2,0,1:T(8,128)(2,1)S(1)}, u32[]{:S(2)}, u32[]{:S(2)}) %collective-permute-start.4) | collective-permute-done | bytes 65568 | tf_op jit(solution)/shard_map/while/body/eval_jaxpr/ppermute | solution.py:24
  318.2 98.9 %while.145 = (s32[]{:T(128)}, bf16[128,4,128]{2,0,1:T(8,128)(2,1)S(1)}, bf16[128,4,128]{2,0,1:T(8,128)(2,1)S(1)}, f32[128,4]{0,1:T(4,128)S(1)}, f32[128,4]{0,1:T...) while((s32[]{:T(128)}, ...), condition=%wide.region_14.15_spmd, body=%wide.region_11.14_spmd.sunk | while | flops 52327952 | bytes 4272506 | solution.py:121
  319.3 9.8 %collective-permute-done.2 = bf16[128,4,128]{2,0,1:T(8,128)(2,1)S(1)} collective-permute-done((bf16[128,4,128]{2,0,1:T(8,128)(2,1)S(1)}, bf16[128,4,128]{2,0,1:T(8,128)(2,1)S(1)}, u32[]{:S(2)}, u32[]{:S(2)}) %collective-permute-start.2) | collective-permute-done | bytes 131104 | tf_op jit(solution)/shard_map/while/body/eval_jaxpr/ppermute | solution.py:24
  333.3 9.8 %collective-permute-done.2 = bf16[128,4,128]{2,0,1:T(8,128)(2,1)S(1)} collective-permute-done((bf16[128,4,128]{2,0,1:T(8,128)(2,1)S(1)}, bf16[128,4,128]{2,0,1:T(8,128)(2,1)S(1)}, u32[]{:S(2)}, u32[]{:S(2)}) %collective-permute-start.2) | collective-permute-done | bytes 131104 | tf_op jit(solution)/shard_map/while/body/eval_jaxpr/ppermute | solution.py:24
  347.4 9.8 %collective-permute-done.2 = bf16[128,4,128]{2,0,1:T(8,128)(2,1)S(1)} collective-permute-done((bf16[128,4,128]{2,0,1:T(8,128)(2,1)S(1)}, bf16[128,4,128]{2,0,1:T(8,128)(2,1)S(1)}, u32[]{:S(2)}, u32[]{:S(2)}) %collective-permute-start.2) | collective-permute-done | bytes 131104 | tf_op jit(solution)/shard_map/while/body/eval_jaxpr/ppermute | solution.py:24
  361.4 9.8 %collective-permute-done.2 = bf16[128,4,128]{2,0,1:T(8,128)(2,1)S(1)} collective-permute-done((bf16[128,4,128]{2,0,1:T(8,128)(2,1)S(1)}, bf16[128,4,128]{2,0,1:T(8,128)(2,1)S(1)}, u32[]{:S(2)}, u32[]{:S(2)}) %collective-permute-start.2) | collective-permute-done | bytes 131104 | tf_op jit(solution)/shard_map/while/body/eval_jaxpr/ppermute | solution.py:24
  375.4 9.8 %collective-permute-done.2 = bf16[128,4,128]{2,0,1:T(8,128)(2,1)S(1)} collective-permute-done((bf16[128,4,128]{2,0,1:T(8,128)(2,1)S(1)}, bf16[128,4,128]{2,0,1:T(8,128)(2,1)S(1)}, u32[]{:S(2)}, u32[]{:S(2)}) %collective-permute-start.2) | collective-permute-done | bytes 131104 | tf_op jit(solution)/shard_map/while/body/eval_jaxpr/ppermute | solution.py:24
  390.1 9.8 %collective-permute-done.2 = bf16[128,4,128]{2,0,1:T(8,128)(2,1)S(1)} collective-permute-done((bf16[128,4,128]{2,0,1:T(8,128)(2,1)S(1)}, bf16[128,4,128]{2,0,1:T(8,128)(2,1)S(1)}, u32[]{:S(2)}, u32[]{:S(2)}) %collective-permute-start.2) | collective-permute-done | bytes 131104 | tf_op jit(solution)/shard_map/while/body/eval_jaxpr/ppermute | solution.py:24
  404.1 9.8 %collective-permute-done.2 = bf16[128,4,128]{2,0,1:T(8,128)(2,1)S(1)} collective-permute-done((bf16[128,4,128]{2,0,1:T(8,128)(2,1)S(1)}, bf16[128,4,128]{2,0,1:T(8,128)(2,1)S(1)}, u32[]{:S(2)}, u32[]{:S(2)}) %collective-permute-start.2) | collective-permute-done | bytes 131104 | tf_op jit(solution)/shard_map/while/body/eval_jaxpr/ppermute | solution.py:24
  457.5 74.9 %while.147 = (s32[]{:T(128)}, bf16[256,4,128]{2,0,1:T(8,128)(2,1)S(1)}, bf16[256,4,128]{2,0,1:T(8,128)(2,1)S(1)}, bf16[256,4,128]{2,0,1:T(8,128)(2,1)}, bf16[256...) while((s32[]{:T(128)}, ...), condition=%wide.region_26.27_spmd, body=%wide.region_25.26_spmd.sunk | while | flops 339403264 | bytes 13939170 | solution.py:182
  458.7 13.9 %collective-permute-done.6 = bf16[256,4,128]{2,0,1:T(8,128)(2,1)S(1)} collective-permute-done((bf16[256,4,128]{2,0,1:T(8,128)(2,1)S(1)}, bf16[256,4,128]{2,0,1:T(8,128)(2,1)S(1)}, u32[]{:S(2)}, u32[]{:S(2)}) %collective-permute-start.6) | collective-permute-done | bytes 262176 | tf_op jit(solution)/shard_map/while/body/eval_jaxpr/ppermute | solution.py:24
  484.7 14.1 %collective-permute-done.6 = bf16[256,4,128]{2,0,1:T(8,128)(2,1)S(1)} collective-permute-done((bf16[256,4,128]{2,0,1:T(8,128)(2,1)S(1)}, bf16[256,4,128]{2,0,1:T(8,128)(2,1)S(1)}, u32[]{:S(2)}, u32[]{:S(2)}) %collective-permute-start.6) | collective-permute-done | bytes 262176 | tf_op jit(solution)/shard_map/while/body/eval_jaxpr/ppermute | solution.py:24
  510.0 11.4 %collective-permute-done.6 = bf16[256,4,128]{2,0,1:T(8,128)(2,1)S(1)} collective-permute-done((bf16[256,4,128]{2,0,1:T(8,128)(2,1)S(1)}, bf16[256,4,128]{2,0,1:T(8,128)(2,1)S(1)}, u32[]{:S(2)}, u32[]{:S(2)}) %collective-permute-start.6) | collective-permute-done | bytes 262176 | tf_op jit(solution)/shard_map/while/body/eval_jaxpr/ppermute | solution.py:24
  534.8 134.4 %while.148 = (s32[]{:T(128)}, bf16[128,4,128]{2,0,1:T(8,128)(2,1)}, bf16[128,4,128]{2,0,1:T(8,128)(2,1)S(1)}, bf16[128,4,128]{2,0,1:T(8,128)(2,1)}, bf16[128,4,1...) while((s32[]{:T(128)}, bf16[128,4,128]{2,0,1:T(8,128)(2,1)}, ...), condition=%wide.region_31.32_spmd, body=%wide.region_30.31_spmd.sunk | while | flops 85094928 | bytes 5790178 | solution.py:182
  557.4 11.4 %collective-permute-done.10 = bf16[128,4,128]{2,0,1:T(8,128)(2,1)S(1)} collective-permute-done((bf16[128,4,128]{2,0,1:T(8,128)(2,1)}, bf16[128,4,128]{2,0,1:T(8,128)(2,1)S(1)}, u32[]{:S(2)}, u32[]{:S(2)}) %collective-permute-start.10) | collective-permute-done | bytes 131104 | tf_op jit(solution)/shard_map/while/body/eval_jaxpr/ppermute | solution.py:24
  578.2 11.5 %collective-permute-done.10 = bf16[128,4,128]{2,0,1:T(8,128)(2,1)S(1)} collective-permute-done((bf16[128,4,128]{2,0,1:T(8,128)(2,1)}, bf16[128,4,128]{2,0,1:T(8,128)(2,1)S(1)}, u32[]{:S(2)}, u32[]{:S(2)}) %collective-permute-start.10) | collective-permute-done | bytes 131104 | tf_op jit(solution)/shard_map/while/body/eval_jaxpr/ppermute | solution.py:24
  598.1 11.5 %collective-permute-done.10 = bf16[128,4,128]{2,0,1:T(8,128)(2,1)S(1)} collective-permute-done((bf16[128,4,128]{2,0,1:T(8,128)(2,1)}, bf16[128,4,128]{2,0,1:T(8,128)(2,1)S(1)}, u32[]{:S(2)}, u32[]{:S(2)}) %collective-permute-start.10) | collective-permute-done | bytes 131104 | tf_op jit(solution)/shard_map/while/body/eval_jaxpr/ppermute | solution.py:24
  617.1 11.5 %collective-permute-done.10 = bf16[128,4,128]{2,0,1:T(8,128)(2,1)S(1)} collective-permute-done((bf16[128,4,128]{2,0,1:T(8,128)(2,1)}, bf16[128,4,128]{2,0,1:T(8,128)(2,1)S(1)}, u32[]{:S(2)}, u32[]{:S(2)}) %collective-permute-start.10) | collective-permute-done | bytes 131104 | tf_op jit(solution)/shard_map/while/body/eval_jaxpr/ppermute | solution.py:24
  635.2 10.1 %collective-permute-done.10 = bf16[128,4,128]{2,0,1:T(8,128)(2,1)S(1)} collective-permute-done((bf16[128,4,128]{2,0,1:T(8,128)(2,1)}, bf16[128,4,128]{2,0,1:T(8,128)(2,1)S(1)}, u32[]{:S(2)}, u32[]{:S(2)}) %collective-permute-start.10) | collective-permute-done | bytes 131104 | tf_op jit(solution)/shard_map/while/body/eval_jaxpr/ppermute | solution.py:24
  651.2 10.1 %collective-permute-done.10 = bf16[128,4,128]{2,0,1:T(8,128)(2,1)S(1)} collective-permute-done((bf16[128,4,128]{2,0,1:T(8,128)(2,1)}, bf16[128,4,128]{2,0,1:T(8,128)(2,1)S(1)}, u32[]{:S(2)}, u32[]{:S(2)}) %collective-permute-start.10) | collective-permute-done | bytes 131104 | tf_op jit(solution)/shard_map/while/body/eval_jaxpr/ppermute | solution.py:24
  669.3 194.8 %while.149 = (s32[]{:T(128)}, bf16[64,4,128]{2,0,1:T(8,128)(2,1)S(1)}, bf16[64,4,128]{2,0,1:T(8,128)(2,1)S(1)}, bf16[64,4,128]{2,0,1:T(8,128)(2,1)S(1)}, bf16[64...) while((s32[]{:T(128)}, ...), condition=%wide.region_36.37_spmd, body=%wide.region_35.36_spmd.sunk | while | flops 21395728 | bytes 2600418 | solution.py:182
  669.8 10.0 %collective-permute-done.14 = bf16[64,4,128]{2,0,1:T(8,128)(2,1)S(1)} collective-permute-done((bf16[64,4,128]{2,0,1:T(8,128)(2,1)S(1)}, bf16[64,4,128]{2,0,1:T(8,128)(2,1)S(1)}, u32[]{:S(2)}, u32[]{:S(2)}) %collective-permute-start.14) | collective-permute-done | bytes 65568 | tf_op jit(solution)/shard_map/while/body/eval_jaxpr/ppermute | solution.py:24
  682.7 9.6 %collective-permute-done.14 = bf16[64,4,128]{2,0,1:T(8,128)(2,1)S(1)} collective-permute-done((bf16[64,4,128]{2,0,1:T(8,128)(2,1)S(1)}, bf16[64,4,128]{2,0,1:T(8,128)(2,1)S(1)}, u32[]{:S(2)}, u32[]{:S(2)}) %collective-permute-start.14) | collective-permute-done | bytes 65568 | tf_op jit(solution)/shard_map/while/body/eval_jaxpr/ppermute | solution.py:24
  695.1 9.6 %collective-permute-done.14 = bf16[64,4,128]{2,0,1:T(8,128)(2,1)S(1)} collective-permute-done((bf16[64,4,128]{2,0,1:T(8,128)(2,1)S(1)}, bf16[64,4,128]{2,0,1:T(8,128)(2,1)S(1)}, u32[]{:S(2)}, u32[]{:S(2)}) %collective-permute-start.14) | collective-permute-done | bytes 65568 | tf_op jit(solution)/shard_map/while/body/eval_jaxpr/ppermute | solution.py:24
  707.5 9.6 %collective-permute-done.14 = bf16[64,4,128]{2,0,1:T(8,128)(2,1)S(1)} collective-permute-done((bf16[64,4,128]{2,0,1:T(8,128)(2,1)S(1)}, bf16[64,4,128]{2,0,1:T(8,128)(2,1)S(1)}, u32[]{:S(2)}, u32[]{:S(2)}) %collective-permute-start.14) | collective-permute-done | bytes 65568 | tf_op jit(solution)/shard_map/while/body/eval_jaxpr/ppermute | solution.py:24
  719.9 9.6 %collective-permute-done.14 = bf16[64,4,128]{2,0,1:T(8,128)(2,1)S(1)} collective-permute-done((bf16[64,4,128]{2,0,1:T(8,128)(2,1)S(1)}, bf16[64,4,128]{2,0,1:T(8,128)(2,1)S(1)}, u32[]{:S(2)}, u32[]{:S(2)}) %collective-permute-start.14) | collective-permute-done | bytes 65568 | tf_op jit(solution)/shard_map/while/body/eval_jaxpr/ppermute | solution.py:24
  732.3 9.6 %collective-permute-done.14 = bf16[64,4,128]{2,0,1:T(8,128)(2,1)S(1)} collective-permute-done((bf16[64,4,128]{2,0,1:T(8,128)(2,1)S(1)}, bf16[64,4,128]{2,0,1:T(8,128)(2,1)S(1)}, u32[]{:S(2)}, u32[]{:S(2)}) %collective-permute-start.14) | collective-permute-done | bytes 65568 | tf_op jit(solution)/shard_map/while/body/eval_jaxpr/ppermute | solution.py:24
  744.7 9.6 %collective-permute-done.14 = bf16[64,4,128]{2,0,1:T(8,128)(2,1)S(1)} collective-permute-done((bf16[64,4,128]{2,0,1:T(8,128)(2,1)S(1)}, bf16[64,4,128]{2,0,1:T(8,128)(2,1)S(1)}, u32[]{:S(2)}, u32[]{:S(2)}) %collective-permute-start.14) | collective-permute-done | bytes 65568 | tf_op jit(solution)/shard_map/while/body/eval_jaxpr/ppermute | solution.py:24
  757.6 9.6 %collective-permute-done.14 = bf16[64,4,128]{2,0,1:T(8,128)(2,1)S(1)} collective-permute-done((bf16[64,4,128]{2,0,1:T(8,128)(2,1)S(1)}, bf16[64,4,128]{2,0,1:T(8,128)(2,1)S(1)}, u32[]{:S(2)}, u32[]{:S(2)}) %collective-permute-start.14) | collective-permute-done | bytes 65568 | tf_op jit(solution)/shard_map/while/body/eval_jaxpr/ppermute | solution.py:24
  771.6 10.2 %collective-permute-done.14 = bf16[64,4,128]{2,0,1:T(8,128)(2,1)S(1)} collective-permute-done((bf16[64,4,128]{2,0,1:T(8,128)(2,1)S(1)}, bf16[64,4,128]{2,0,1:T(8,128)(2,1)S(1)}, u32[]{:S(2)}, u32[]{:S(2)}) %collective-permute-start.14) | collective-permute-done | bytes 65568 | tf_op jit(solution)/shard_map/while/body/eval_jaxpr/ppermute | solution.py:24
  786.8 10.3 %collective-permute-done.14 = bf16[64,4,128]{2,0,1:T(8,128)(2,1)S(1)} collective-permute-done((bf16[64,4,128]{2,0,1:T(8,128)(2,1)S(1)}, bf16[64,4,128]{2,0,1:T(8,128)(2,1)S(1)}, u32[]{:S(2)}, u32[]{:S(2)}) %collective-permute-start.14) | collective-permute-done | bytes 65568 | tf_op jit(solution)/shard_map/while/body/eval_jaxpr/ppermute | solution.py:24
  801.1 10.3 %collective-permute-done.14 = bf16[64,4,128]{2,0,1:T(8,128)(2,1)S(1)} collective-permute-done((bf16[64,4,128]{2,0,1:T(8,128)(2,1)S(1)}, bf16[64,4,128]{2,0,1:T(8,128)(2,1)S(1)}, u32[]{:S(2)}, u32[]{:S(2)}) %collective-permute-start.14) | collective-permute-done | bytes 65568 | tf_op jit(solution)/shard_map/while/body/eval_jaxpr/ppermute | solution.py:24
  814.7 9.6 %collective-permute-done.14 = bf16[64,4,128]{2,0,1:T(8,128)(2,1)S(1)} collective-permute-done((bf16[64,4,128]{2,0,1:T(8,128)(2,1)S(1)}, bf16[64,4,128]{2,0,1:T(8,128)(2,1)S(1)}, u32[]{:S(2)}, u32[]{:S(2)}) %collective-permute-start.14) | collective-permute-done | bytes 65568 | tf_op jit(solution)/shard_map/while/body/eval_jaxpr/ppermute | solution.py:24
  827.4 9.6 %collective-permute-done.14 = bf16[64,4,128]{2,0,1:T(8,128)(2,1)S(1)} collective-permute-done((bf16[64,4,128]{2,0,1:T(8,128)(2,1)S(1)}, bf16[64,4,128]{2,0,1:T(8,128)(2,1)S(1)}, u32[]{:S(2)}, u32[]{:S(2)}) %collective-permute-start.14) | collective-permute-done | bytes 65568 | tf_op jit(solution)/shard_map/while/body/eval_jaxpr/ppermute | solution.py:24
  839.8 9.6 %collective-permute-done.14 = bf16[64,4,128]{2,0,1:T(8,128)(2,1)S(1)} collective-permute-done((bf16[64,4,128]{2,0,1:T(8,128)(2,1)S(1)}, bf16[64,4,128]{2,0,1:T(8,128)(2,1)S(1)}, u32[]{:S(2)}, u32[]{:S(2)}) %collective-permute-start.14) | collective-permute-done | bytes 65568 | tf_op jit(solution)/shard_map/while/body/eval_jaxpr/ppermute | solution.py:24
  852.2 9.6 %collective-permute-done.14 = bf16[64,4,128]{2,0,1:T(8,128)(2,1)S(1)} collective-permute-done((bf16[64,4,128]{2,0,1:T(8,128)(2,1)S(1)}, bf16[64,4,128]{2,0,1:T(8,128)(2,1)S(1)}, u32[]{:S(2)}, u32[]{:S(2)}) %collective-permute-start.14) | collective-permute-done | bytes 65568 | tf_op jit(solution)/shard_map/while/body/eval_jaxpr/ppermute | solution.py:24
  (1162 shorter events, 429.3 us)
Async XLA Ops:
  7.2 35.5 %all-gather.2.cloned.1.call-start = ((), (), s32[]{:S(2)}) async-start(), calls=%async_computation | async-start | bytes 2621440 | tf_op jit(solution)/shard_map/all_gather | solution.py:210
  69.5 15.4 %collective-permute-start = (bf16[256,4,128]{2,0,1:T(8,128)(2,1)}, bf16[256,4,128]{2,0,1:T(8,128)(2,1)S(1)}, u32[]{:S(2)}, u32[]{:S(2)}) collective-permute-start(bf16[256,4,128]{2,0,1:T(8,128)(2,1)} %get-tuple-element.3054), channel_id=1, source_target_pairs={{252,0},{0,4},{4,8},{8,12},{12,16},{16,20},{20,24},{24,28},{28,32}... | collective-permute-start | bytes 786440 | tf_op jit(solution)/shard_map/while/body/eval_jaxpr/ppermute | solution.py:24
  71.8 18.5 %collective-permute-start.1 = (bf16[256,4,128]{2,0,1:T(8,128)(2,1)}, bf16[256,4,128]{2,0,1:T(8,128)(2,1)S(1)}, u32[]{:S(2)}, u32[]{:S(2)}) collective-permute-start(bf16[256,4,128]{2,0,1:T(8,128)(2,1)} %get-tuple-element.3055), channel_id=1, source_target_pairs={{252,0},{0,4},{4,8},{8,12},{12,16},{16,20},{20,24},{24,28},{28,32}... | collective-permute-start | bytes 786440 | tf_op jit(solution)/shard_map/while/body/eval_jaxpr/ppermute | solution.py:24
  94.4 15.2 %collective-permute-start = (bf16[256,4,128]{2,0,1:T(8,128)(2,1)}, bf16[256,4,128]{2,0,1:T(8,128)(2,1)S(1)}, u32[]{:S(2)}, u32[]{:S(2)}) collective-permute-start(bf16[256,4,128]{2,0,1:T(8,128)(2,1)} %get-tuple-element.3054), channel_id=1, source_target_pairs={{252,0},{0,4},{4,8},{8,12},{12,16},{16,20},{20,24},{24,28},{28,32}... | collective-permute-start | bytes 786440 | tf_op jit(solution)/shard_map/while/body/eval_jaxpr/ppermute | solution.py:24
  94.4 19.6 %collective-permute-start.1 = (bf16[256,4,128]{2,0,1:T(8,128)(2,1)}, bf16[256,4,128]{2,0,1:T(8,128)(2,1)S(1)}, u32[]{:S(2)}, u32[]{:S(2)}) collective-permute-start(bf16[256,4,128]{2,0,1:T(8,128)(2,1)} %get-tuple-element.3055), channel_id=1, source_target_pairs={{252,0},{0,4},{4,8},{8,12},{12,16},{16,20},{20,24},{24,28},{28,32}... | collective-permute-start | bytes 786440 | tf_op jit(solution)/shard_map/while/body/eval_jaxpr/ppermute | solution.py:24
  118.2 15.3 %collective-permute-start = (bf16[256,4,128]{2,0,1:T(8,128)(2,1)}, bf16[256,4,128]{2,0,1:T(8,128)(2,1)S(1)}, u32[]{:S(2)}, u32[]{:S(2)}) collective-permute-start(bf16[256,4,128]{2,0,1:T(8,128)(2,1)} %get-tuple-element.3054), channel_id=1, source_target_pairs={{252,0},{0,4},{4,8},{8,12},{12,16},{16,20},{20,24},{24,28},{28,32}... | collective-permute-start | bytes 786440 | tf_op jit(solution)/shard_map/while/body/eval_jaxpr/ppermute | solution.py:24
  118.3 18.7 %collective-permute-start.1 = (bf16[256,4,128]{2,0,1:T(8,128)(2,1)}, bf16[256,4,128]{2,0,1:T(8,128)(2,1)S(1)}, u32[]{:S(2)}, u32[]{:S(2)}) collective-permute-start(bf16[256,4,128]{2,0,1:T(8,128)(2,1)} %get-tuple-element.3055), channel_id=1, source_target_pairs={{252,0},{0,4},{4,8},{8,12},{12,16},{16,20},{20,24},{24,28},{28,32}... | collective-permute-start | bytes 786440 | tf_op jit(solution)/shard_map/while/body/eval_jaxpr/ppermute | solution.py:24
  374.6 13.2 %collective-permute-start.3 = (bf16[128,4,128]{2,0,1:T(8,128)(2,1)S(1)}, bf16[128,4,128]{2,0,1:T(8,128)(2,1)S(1)}, u32[]{:S(2)}, u32[]{:S(2)}) collective-permute-start(bf16[128,4,128]{2,0,1:T(8,128)(2,1)S(1)} %get-tuple-element.2965), channel_id=1, source_target_pairs={{252,0},{0,4},{4,8},{8,12},{12,16},{16,20},{20,24},{24,28},{28,32}... | collective-permute-start | bytes 393224 | tf_op jit(solution)/shard_map/while/body/eval_jaxpr/ppermute | solution.py:24
  457.5 15.0 %collective-permute-start.6 = (bf16[256,4,128]{2,0,1:T(8,128)(2,1)S(1)}, bf16[256,4,128]{2,0,1:T(8,128)(2,1)S(1)}, u32[]{:S(2)}, u32[]{:S(2)}) collective-permute-start(bf16[256,4,128]{2,0,1:T(8,128)(2,1)S(1)} %get-tuple-element.3156), channel_id=1, source_target_pairs={{252,0},{0,4},{4,8},{8,12},{12,16},{16,20},{20,24},{24,28},{28,32}... | collective-permute-start | bytes 786440 | tf_op jit(solution)/shard_map/while/body/eval_jaxpr/ppermute | solution.py:24
  457.6 19.5 %collective-permute-start.7 = (bf16[256,4,128]{2,0,1:T(8,128)(2,1)S(1)}, bf16[256,4,128]{2,0,1:T(8,128)(2,1)S(1)}, u32[]{:S(2)}, u32[]{:S(2)}) collective-permute-start(bf16[256,4,128]{2,0,1:T(8,128)(2,1)S(1)} %get-tuple-element.3157), channel_id=1, source_target_pairs={{252,0},{0,4},{4,8},{8,12},{12,16},{16,20},{20,24},{24,28},{28,32}... | collective-permute-start | bytes 786440 | tf_op jit(solution)/shard_map/while/body/eval_jaxpr/ppermute | solution.py:24
  457.7 22.3 %collective-permute-start.8 = (bf16[256,4,128]{2,0,1:T(8,128)(2,1)}, bf16[256,4,128]{2,0,1:T(8,128)(2,1)S(1)}, u32[]{:S(2)}, u32[]{:S(2)}) collective-permute-start(bf16[256,4,128]{2,0,1:T(8,128)(2,1)} %get-tuple-element.3158), channel_id=1, source_target_pairs={{252,0},{0,4},{4,8},{8,12},{12,16},{16,20},{20,24},{24,28},{28,32}... | collective-permute-start | bytes 786440 | tf_op jit(solution)/shard_map/while/body/eval_jaxpr/ppermute | solution.py:24
  457.8 25.0 %collective-permute-start.9 = (bf16[256,4,128]{2,0,1:T(8,128)(2,1)}, bf16[256,4,128]{2,0,1:T(8,128)(2,1)S(1)}, u32[]{:S(2)}, u32[]{:S(2)}) collective-permute-start(bf16[256,4,128]{2,0,1:T(8,128)(2,1)} %get-tuple-element.3159), channel_id=1, source_target_pairs={{252,0},{0,4},{4,8},{8,12},{12,16},{16,20},{20,24},{24,28},{28,32}... | collective-permute-start | bytes 786440 | tf_op jit(solution)/shard_map/while/body/eval_jaxpr/ppermute | solution.py:24
  483.8 15.0 %collective-permute-start.6 = (bf16[256,4,128]{2,0,1:T(8,128)(2,1)S(1)}, bf16[256,4,128]{2,0,1:T(8,128)(2,1)S(1)}, u32[]{:S(2)}, u32[]{:S(2)}) collective-permute-start(bf16[256,4,128]{2,0,1:T(8,128)(2,1)S(1)} %get-tuple-element.3156), channel_id=1, source_target_pairs={{252,0},{0,4},{4,8},{8,12},{12,16},{16,20},{20,24},{24,28},{28,32}... | collective-permute-start | bytes 786440 | tf_op jit(solution)/shard_map/while/body/eval_jaxpr/ppermute | solution.py:24
  483.8 18.6 %collective-permute-start.7 = (bf16[256,4,128]{2,0,1:T(8,128)(2,1)S(1)}, bf16[256,4,128]{2,0,1:T(8,128)(2,1)S(1)}, u32[]{:S(2)}, u32[]{:S(2)}) collective-permute-start(bf16[256,4,128]{2,0,1:T(8,128)(2,1)S(1)} %get-tuple-element.3157), channel_id=1, source_target_pairs={{252,0},{0,4},{4,8},{8,12},{12,16},{16,20},{20,24},{24,28},{28,32}... | collective-permute-start | bytes 786440 | tf_op jit(solution)/shard_map/while/body/eval_jaxpr/ppermute | solution.py:24
  483.8 21.4 %collective-permute-start.8 = (bf16[256,4,128]{2,0,1:T(8,128)(2,1)}, bf16[256,4,128]{2,0,1:T(8,128)(2,1)S(1)}, u32[]{:S(2)}, u32[]{:S(2)}) collective-permute-start(bf16[256,4,128]{2,0,1:T(8,128)(2,1)} %get-tuple-element.3158), channel_id=1, source_target_pairs={{252,0},{0,4},{4,8},{8,12},{12,16},{16,20},{20,24},{24,28},{28,32}... | collective-permute-start | bytes 786440 | tf_op jit(solution)/shard_map/while/body/eval_jaxpr/ppermute | solution.py:24
  483.9 24.2 %collective-permute-start.9 = (bf16[256,4,128]{2,0,1:T(8,128)(2,1)}, bf16[256,4,128]{2,0,1:T(8,128)(2,1)S(1)}, u32[]{:S(2)}, u32[]{:S(2)}) collective-permute-start(bf16[256,4,128]{2,0,1:T(8,128)(2,1)} %get-tuple-element.3159), channel_id=1, source_target_pairs={{252,0},{0,4},{4,8},{8,12},{12,16},{16,20},{20,24},{24,28},{28,32}... | collective-permute-start | bytes 786440 | tf_op jit(solution)/shard_map/while/body/eval_jaxpr/ppermute | solution.py:24
  509.1 15.1 %collective-permute-start.7 = (bf16[256,4,128]{2,0,1:T(8,128)(2,1)S(1)}, bf16[256,4,128]{2,0,1:T(8,128)(2,1)S(1)}, u32[]{:S(2)}, u32[]{:S(2)}) collective-permute-start(bf16[256,4,128]{2,0,1:T(8,128)(2,1)S(1)} %get-tuple-element.3157), channel_id=1, source_target_pairs={{252,0},{0,4},{4,8},{8,12},{12,16},{16,20},{20,24},{24,28},{28,32}... | collective-permute-start | bytes 786440 | tf_op jit(solution)/shard_map/while/body/eval_jaxpr/ppermute | solution.py:24
  509.1 17.9 %collective-permute-start.8 = (bf16[256,4,128]{2,0,1:T(8,128)(2,1)}, bf16[256,4,128]{2,0,1:T(8,128)(2,1)S(1)}, u32[]{:S(2)}, u32[]{:S(2)}) collective-permute-start(bf16[256,4,128]{2,0,1:T(8,128)(2,1)} %get-tuple-element.3158), channel_id=1, source_target_pairs={{252,0},{0,4},{4,8},{8,12},{12,16},{16,20},{20,24},{24,28},{28,32}... | collective-permute-start | bytes 786440 | tf_op jit(solution)/shard_map/while/body/eval_jaxpr/ppermute | solution.py:24
  509.1 22.2 %collective-permute-start.9 = (bf16[256,4,128]{2,0,1:T(8,128)(2,1)}, bf16[256,4,128]{2,0,1:T(8,128)(2,1)S(1)}, u32[]{:S(2)}, u32[]{:S(2)}) collective-permute-start(bf16[256,4,128]{2,0,1:T(8,128)(2,1)} %get-tuple-element.3159), channel_id=1, source_target_pairs={{252,0},{0,4},{4,8},{8,12},{12,16},{16,20},{20,24},{24,28},{28,32}... | collective-permute-start | bytes 786440 | tf_op jit(solution)/shard_map/while/body/eval_jaxpr/ppermute | solution.py:24
  533.5 350.4 %collective-permute-start.18 = (bf16[256,4,128]{0,2,1:T(8,128)(2,1)S(1)}, bf16[256,4,128]{0,2,1:T(8,128)(2,1)}, u32[]{:S(2)}, u32[]{:S(2)}) collective-permute-start(bf16[256,4,128]{0,2,1:T(8,128)(2,1)S(1)} %copy.528), channel_id=1, source_target_pairs={{12,0},{16,4},{20,8},{24,12},{28,16},{32,20},{36,24},{40,28},{44,3... | collective-permute-start | bytes 786440 | tf_op jit(solution)/shard_map/ppermute | solution.py:24
  535.7 14.4 %collective-permute-start.11 = (bf16[128,4,128]{2,0,1:T(8,128)(2,1)S(1)}, bf16[128,4,128]{2,0,1:T(8,128)(2,1)S(1)}, u32[]{:S(2)}, u32[]{:S(2)}) collective-permute-start(bf16[128,4,128]{2,0,1:T(8,128)(2,1)S(1)} %get-tuple-element.3211), channel_id=1, source_target_pairs={{252,0},{0,4},{4,8},{8,12},{12,16},{16,20},{20,24},{24,28},{28,32}... | collective-permute-start | bytes 393224 | tf_op jit(solution)/shard_map/while/body/eval_jaxpr/ppermute | solution.py:24
  537.6 15.3 %collective-permute-start.12 = (bf16[128,4,128]{2,0,1:T(8,128)(2,1)}, bf16[128,4,128]{2,0,1:T(8,128)(2,1)S(1)}, u32[]{:S(2)}, u32[]{:S(2)}) collective-permute-start(bf16[128,4,128]{2,0,1:T(8,128)(2,1)} %get-tuple-element.3212), channel_id=1, source_target_pairs={{252,0},{0,4},{4,8},{8,12},{12,16},{16,20},{20,24},{24,28},{28,32}... | collective-permute-start | bytes 393224 | tf_op jit(solution)/shard_map/while/body/eval_jaxpr/ppermute | solution.py:24
  540.0 15.7 %collective-permute-start.13 = (bf16[128,4,128]{2,0,1:T(8,128)(2,1)}, bf16[128,4,128]{2,0,1:T(8,128)(2,1)S(1)}, u32[]{:S(2)}, u32[]{:S(2)}) collective-permute-start(bf16[128,4,128]{2,0,1:T(8,128)(2,1)} %get-tuple-element.3213), channel_id=1, source_target_pairs={{252,0},{0,4},{4,8},{8,12},{12,16},{16,20},{20,24},{24,28},{28,32}... | collective-permute-start | bytes 393224 | tf_op jit(solution)/shard_map/while/body/eval_jaxpr/ppermute | solution.py:24
  556.6 15.1 %collective-permute-start.11 = (bf16[128,4,128]{2,0,1:T(8,128)(2,1)S(1)}, bf16[128,4,128]{2,0,1:T(8,128)(2,1)S(1)}, u32[]{:S(2)}, u32[]{:S(2)}) collective-permute-start(bf16[128,4,128]{2,0,1:T(8,128)(2,1)S(1)} %get-tuple-element.3211), channel_id=1, source_target_pairs={{252,0},{0,4},{4,8},{8,12},{12,16},{16,20},{20,24},{24,28},{28,32}... | collective-permute-start | bytes 393224 | tf_op jit(solution)/shard_map/while/body/eval_jaxpr/ppermute | solution.py:24
  556.6 17.9 %collective-permute-start.12 = (bf16[128,4,128]{2,0,1:T(8,128)(2,1)}, bf16[128,4,128]{2,0,1:T(8,128)(2,1)S(1)}, u32[]{:S(2)}, u32[]{:S(2)}) collective-permute-start(bf16[128,4,128]{2,0,1:T(8,128)(2,1)} %get-tuple-element.3212), channel_id=1, source_target_pairs={{252,0},{0,4},{4,8},{8,12},{12,16},{16,20},{20,24},{24,28},{28,32}... | collective-permute-start | bytes 393224 | tf_op jit(solution)/shard_map/while/body/eval_jaxpr/ppermute | solution.py:24
  556.6 19.9 %collective-permute-start.13 = (bf16[128,4,128]{2,0,1:T(8,128)(2,1)}, bf16[128,4,128]{2,0,1:T(8,128)(2,1)S(1)}, u32[]{:S(2)}, u32[]{:S(2)}) collective-permute-start(bf16[128,4,128]{2,0,1:T(8,128)(2,1)} %get-tuple-element.3213), channel_id=1, source_target_pairs={{252,0},{0,4},{4,8},{8,12},{12,16},{16,20},{20,24},{24,28},{28,32}... | collective-permute-start | bytes 393224 | tf_op jit(solution)/shard_map/while/body/eval_jaxpr/ppermute | solution.py:24
  577.4 15.2 %collective-permute-start.11 = (bf16[128,4,128]{2,0,1:T(8,128)(2,1)S(1)}, bf16[128,4,128]{2,0,1:T(8,128)(2,1)S(1)}, u32[]{:S(2)}, u32[]{:S(2)}) collective-permute-start(bf16[128,4,128]{2,0,1:T(8,128)(2,1)S(1)} %get-tuple-element.3211), channel_id=1, source_target_pairs={{252,0},{0,4},{4,8},{8,12},{12,16},{16,20},{20,24},{24,28},{28,32}... | collective-permute-start | bytes 393224 | tf_op jit(solution)/shard_map/while/body/eval_jaxpr/ppermute | solution.py:24
  577.4 17.6 %collective-permute-start.12 = (bf16[128,4,128]{2,0,1:T(8,128)(2,1)}, bf16[128,4,128]{2,0,1:T(8,128)(2,1)S(1)}, u32[]{:S(2)}, u32[]{:S(2)}) collective-permute-start(bf16[128,4,128]{2,0,1:T(8,128)(2,1)} %get-tuple-element.3212), channel_id=1, source_target_pairs={{252,0},{0,4},{4,8},{8,12},{12,16},{16,20},{20,24},{24,28},{28,32}... | collective-permute-start | bytes 393224 | tf_op jit(solution)/shard_map/while/body/eval_jaxpr/ppermute | solution.py:24
  577.4 19.0 %collective-permute-start.13 = (bf16[128,4,128]{2,0,1:T(8,128)(2,1)}, bf16[128,4,128]{2,0,1:T(8,128)(2,1)S(1)}, u32[]{:S(2)}, u32[]{:S(2)}) collective-permute-start(bf16[128,4,128]{2,0,1:T(8,128)(2,1)} %get-tuple-element.3213), channel_id=1, source_target_pairs={{252,0},{0,4},{4,8},{8,12},{12,16},{16,20},{20,24},{24,28},{28,32}... | collective-permute-start | bytes 393224 | tf_op jit(solution)/shard_map/while/body/eval_jaxpr/ppermute | solution.py:24
  597.3 15.2 %collective-permute-start.11 = (bf16[128,4,128]{2,0,1:T(8,128)(2,1)S(1)}, bf16[128,4,128]{2,0,1:T(8,128)(2,1)S(1)}, u32[]{:S(2)}, u32[]{:S(2)}) collective-permute-start(bf16[128,4,128]{2,0,1:T(8,128)(2,1)S(1)} %get-tuple-element.3211), channel_id=1, source_target_pairs={{252,0},{0,4},{4,8},{8,12},{12,16},{16,20},{20,24},{24,28},{28,32}... | collective-permute-start | bytes 393224 | tf_op jit(solution)/shard_map/while/body/eval_jaxpr/ppermute | solution.py:24
  597.3 16.7 %collective-permute-start.12 = (bf16[128,4,128]{2,0,1:T(8,128)(2,1)}, bf16[128,4,128]{2,0,1:T(8,128)(2,1)S(1)}, u32[]{:S(2)}, u32[]{:S(2)}) collective-permute-start(bf16[128,4,128]{2,0,1:T(8,128)(2,1)} %get-tuple-element.3212), channel_id=1, source_target_pairs={{252,0},{0,4},{4,8},{8,12},{12,16},{16,20},{20,24},{24,28},{28,32}... | collective-permute-start | bytes 393224 | tf_op jit(solution)/shard_map/while/body/eval_jaxpr/ppermute | solution.py:24
  597.3 18.1 %collective-permute-start.13 = (bf16[128,4,128]{2,0,1:T(8,128)(2,1)}, bf16[128,4,128]{2,0,1:T(8,128)(2,1)S(1)}, u32[]{:S(2)}, u32[]{:S(2)}) collective-permute-start(bf16[128,4,128]{2,0,1:T(8,128)(2,1)} %get-tuple-element.3213), channel_id=1, source_target_pairs={{252,0},{0,4},{4,8},{8,12},{12,16},{16,20},{20,24},{24,28},{28,32}... | collective-permute-start | bytes 393224 | tf_op jit(solution)/shard_map/while/body/eval_jaxpr/ppermute | solution.py:24
  616.3 14.4 %collective-permute-start.11 = (bf16[128,4,128]{2,0,1:T(8,128)(2,1)S(1)}, bf16[128,4,128]{2,0,1:T(8,128)(2,1)S(1)}, u32[]{:S(2)}, u32[]{:S(2)}) collective-permute-start(bf16[128,4,128]{2,0,1:T(8,128)(2,1)S(1)} %get-tuple-element.3211), channel_id=1, source_target_pairs={{252,0},{0,4},{4,8},{8,12},{12,16},{16,20},{20,24},{24,28},{28,32}... | collective-permute-start | bytes 393224 | tf_op jit(solution)/shard_map/while/body/eval_jaxpr/ppermute | solution.py:24
  616.3 15.9 %collective-permute-start.12 = (bf16[128,4,128]{2,0,1:T(8,128)(2,1)}, bf16[128,4,128]{2,0,1:T(8,128)(2,1)S(1)}, u32[]{:S(2)}, u32[]{:S(2)}) collective-permute-start(bf16[128,4,128]{2,0,1:T(8,128)(2,1)} %get-tuple-element.3212), channel_id=1, source_target_pairs={{252,0},{0,4},{4,8},{8,12},{12,16},{16,20},{20,24},{24,28},{28,32}... | collective-permute-start | bytes 393224 | tf_op jit(solution)/shard_map/while/body/eval_jaxpr/ppermute | solution.py:24
  616.3 17.2 %collective-permute-start.13 = (bf16[128,4,128]{2,0,1:T(8,128)(2,1)}, bf16[128,4,128]{2,0,1:T(8,128)(2,1)S(1)}, u32[]{:S(2)}, u32[]{:S(2)}) collective-permute-start(bf16[128,4,128]{2,0,1:T(8,128)(2,1)} %get-tuple-element.3213), channel_id=1, source_target_pairs={{252,0},{0,4},{4,8},{8,12},{12,16},{16,20},{20,24},{24,28},{28,32}... | collective-permute-start | bytes 393224 | tf_op jit(solution)/shard_map/while/body/eval_jaxpr/ppermute | solution.py:24
  634.4 13.8 %collective-permute-start.12 = (bf16[128,4,128]{2,0,1:T(8,128)(2,1)}, bf16[128,4,128]{2,0,1:T(8,128)(2,1)S(1)}, u32[]{:S(2)}, u32[]{:S(2)}) collective-permute-start(bf16[128,4,128]{2,0,1:T(8,128)(2,1)} %get-tuple-element.3212), channel_id=1, source_target_pairs={{252,0},{0,4},{4,8},{8,12},{12,16},{16,20},{20,24},{24,28},{28,32}... | collective-permute-start | bytes 393224 | tf_op jit(solution)/shard_map/while/body/eval_jaxpr/ppermute | solution.py:24
  634.4 15.1 %collective-permute-start.13 = (bf16[128,4,128]{2,0,1:T(8,128)(2,1)}, bf16[128,4,128]{2,0,1:T(8,128)(2,1)S(1)}, u32[]{:S(2)}, u32[]{:S(2)}) collective-permute-start(bf16[128,4,128]{2,0,1:T(8,128)(2,1)} %get-tuple-element.3213), channel_id=1, source_target_pairs={{252,0},{0,4},{4,8},{8,12},{12,16},{16,20},{20,24},{24,28},{28,32}... | collective-permute-start | bytes 393224 | tf_op jit(solution)/shard_map/while/body/eval_jaxpr/ppermute | solution.py:24
  650.4 15.8 %collective-permute-start.12 = (bf16[128,4,128]{2,0,1:T(8,128)(2,1)}, bf16[128,4,128]{2,0,1:T(8,128)(2,1)S(1)}, u32[]{:S(2)}, u32[]{:S(2)}) collective-permute-start(bf16[128,4,128]{2,0,1:T(8,128)(2,1)} %get-tuple-element.3212), channel_id=1, source_target_pairs={{252,0},{0,4},{4,8},{8,12},{12,16},{16,20},{20,24},{24,28},{28,32}... | collective-permute-start | bytes 393224 | tf_op jit(solution)/shard_map/while/body/eval_jaxpr/ppermute | solution.py:24
  650.4 17.9 %collective-permute-start.13 = (bf16[128,4,128]{2,0,1:T(8,128)(2,1)}, bf16[128,4,128]{2,0,1:T(8,128)(2,1)S(1)}, u32[]{:S(2)}, u32[]{:S(2)}) collective-permute-start(bf16[128,4,128]{2,0,1:T(8,128)(2,1)} %get-tuple-element.3213), channel_id=1, source_target_pairs={{252,0},{0,4},{4,8},{8,12},{12,16},{16,20},{20,24},{24,28},{28,32}... | collective-permute-start | bytes 393224 | tf_op jit(solution)/shard_map/while/body/eval_jaxpr/ppermute | solution.py:24
  757.3 13.5 %collective-permute-start.16 = (bf16[64,4,128]{2,0,1:T(8,128)(2,1)S(1)}, bf16[64,4,128]{2,0,1:T(8,128)(2,1)S(1)}, u32[]{:S(2)}, u32[]{:S(2)}) collective-permute-start(bf16[64,4,128]{2,0,1:T(8,128)(2,1)S(1)} %get-tuple-element.3104), channel_id=1, source_target_pairs={{252,0},{0,4},{4,8},{8,12},{12,16},{16,20},{20,24},{24,28},{28,32}... | collective-permute-start | bytes 196616 | tf_op jit(solution)/shard_map/while/body/eval_jaxpr/ppermute | solution.py:24
  771.3 13.4 %collective-permute-start.17 = (bf16[64,4,128]{2,0,1:T(8,128)(2,1)S(1)}, bf16[64,4,128]{2,0,1:T(8,128)(2,1)S(1)}, u32[]{:S(2)}, u32[]{:S(2)}) collective-permute-start(bf16[64,4,128]{2,0,1:T(8,128)(2,1)S(1)} %get-tuple-element.3105), channel_id=1, source_target_pairs={{252,0},{0,4},{4,8},{8,12},{12,16},{16,20},{20,24},{24,28},{28,32}... | collective-permute-start | bytes 196616 | tf_op jit(solution)/shard_map/while/body/eval_jaxpr/ppermute | solution.py:24
  771.4 14.7 %collective-permute-start.16 = (bf16[64,4,128]{2,0,1:T(8,128)(2,1)S(1)}, bf16[64,4,128]{2,0,1:T(8,128)(2,1)S(1)}, u32[]{:S(2)}, u32[]{:S(2)}) collective-permute-start(bf16[64,4,128]{2,0,1:T(8,128)(2,1)S(1)} %get-tuple-element.3104), channel_id=1, source_target_pairs={{252,0},{0,4},{4,8},{8,12},{12,16},{16,20},{20,24},{24,28},{28,32}... | collective-permute-start | bytes 196616 | tf_op jit(solution)/shard_map/while/body/eval_jaxpr/ppermute | solution.py:24
  786.5 13.2 %collective-permute-start.17 = (bf16[64,4,128]{2,0,1:T(8,128)(2,1)S(1)}, bf16[64,4,128]{2,0,1:T(8,128)(2,1)S(1)}, u32[]{:S(2)}, u32[]{:S(2)}) collective-permute-start(bf16[64,4,128]{2,0,1:T(8,128)(2,1)S(1)} %get-tuple-element.3105), channel_id=1, source_target_pairs={{252,0},{0,4},{4,8},{8,12},{12,16},{16,20},{20,24},{24,28},{28,32}... | collective-permute-start | bytes 196616 | tf_op jit(solution)/shard_map/while/body/eval_jaxpr/ppermute | solution.py:24
  786.6 13.9 %collective-permute-start.16 = (bf16[64,4,128]{2,0,1:T(8,128)(2,1)S(1)}, bf16[64,4,128]{2,0,1:T(8,128)(2,1)S(1)}, u32[]{:S(2)}, u32[]{:S(2)}) collective-permute-start(bf16[64,4,128]{2,0,1:T(8,128)(2,1)S(1)} %get-tuple-element.3104), channel_id=1, source_target_pairs={{252,0},{0,4},{4,8},{8,12},{12,16},{16,20},{20,24},{24,28},{28,32}... | collective-permute-start | bytes 196616 | tf_op jit(solution)/shard_map/while/body/eval_jaxpr/ppermute | solution.py:24
  800.9 13.1 %collective-permute-start.16 = (bf16[64,4,128]{2,0,1:T(8,128)(2,1)S(1)}, bf16[64,4,128]{2,0,1:T(8,128)(2,1)S(1)}, u32[]{:S(2)}, u32[]{:S(2)}) collective-permute-start(bf16[64,4,128]{2,0,1:T(8,128)(2,1)S(1)} %get-tuple-element.3104), channel_id=1, source_target_pairs={{252,0},{0,4},{4,8},{8,12},{12,16},{16,20},{20,24},{24,28},{28,32}... | collective-permute-start | bytes 196616 | tf_op jit(solution)/shard_map/while/body/eval_jaxpr/ppermute | solution.py:24
  864.1 19.9 %collective-permute-start.21 = (bf16[256,4,128]{0,2,1:T(8,128)(2,1)S(1)}, bf16[256,4,128]{0,2,1:T(8,128)(2,1)}, u32[]{:S(2)}, u32[]{:S(2)}) collective-permute-start(bf16[256,4,128]{0,2,1:T(8,128)(2,1)S(1)} %copy.534), channel_id=1, source_target_pairs={{12,0},{16,4},{20,8},{24,12},{28,16},{32,20},{36,24},{40,28},{44,3... | collective-permute-start | bytes 786440 | tf_op jit(solution)/shard_map/ppermute | solution.py:24
  867.0 16.7 %collective-permute-start.22 = (bf16[128,4,128]{2,0,1:T(8,128)(2,1)S(1)}, bf16[128,4,128]{2,0,1:T(8,128)(2,1)S(1)}, u32[]{:S(2)}, u32[]{:S(2)}) collective-permute-start(bf16[128,4,128]{2,0,1:T(8,128)(2,1)S(1)} %copy-done.37), channel_id=1, source_target_pairs={{28,0},{32,4},{36,8},{40,12},{44,16},{48,20},{52,24},{56,28},{60,3... | collective-permute-start | bytes 393224 | tf_op jit(solution)/shard_map/ppermute | solution.py:24
  867.0 16.8 %collective-permute-start.19 = (bf16[128,4,128]{2,0,1:T(8,128)(2,1)S(1)}, bf16[128,4,128]{2,0,1:T(8,128)(2,1)S(1)}, u32[]{:S(2)}, u32[]{:S(2)}) collective-permute-start(bf16[128,4,128]{2,0,1:T(8,128)(2,1)S(1)} %copy-done.36), channel_id=1, source_target_pairs={{28,0},{32,4},{36,8},{40,12},{44,16},{48,20},{52,24},{56,28},{60,3... | collective-permute-start | bytes 393224 | tf_op jit(solution)/shard_map/ppermute | solution.py:24
  (197 other events, 6548.8 us)
Sparse Core Ops, SparseCore 0:
  9.8 32.8 all-gather.1
where the time goes:
time: 902 us; the launch traced here: 898 us
  waiting for transfers between devices  624 us (69%)
  matrix products  112 us (12%)
  local copies, waits for them, and re-layouts  60.7 us (7%)
  other arithmetic  57.5 us (6%)
  starting transfers between devices  22.4 us (2%)
  between operations  15.9 us (2%)
    ppermute x156, waiting for transfers between devices, passed_along(): return lax.ppermute(block, axis, route)  601 us
    select_n x53, other arithmetic, linked_pairs(): return (query_pos // segment == key_pos // segment) & (key_pos <= query_pos)  25.9 us
    ppermute x156, starting transfers between devices, passed_along(): return lax.ppermute(block, axis, route)  22.3 us
    all_gather x1, waiting for transfers between devices, local(): lax.all_gather(out_grad, 'tp', axis=1, tiled=True)  21.8 us
  transfers between devices with their start and end apart: 157, of which 144 were waited for; matrix products, arithmetic and copies ran while one was open for 13% of the time, Pallas kernels for 0%

commit v1 on v0

--- a/solution.py
+++ b/solution.py
@@ -8,6 +8,12 @@
 LEVELS = 3
 KEYS_SEG = 1024
 NEGATIVE_FILL = -1e30
+
+
+def members_all_render(arr_in, row_axis):
+    reply = jnp.stack([arr_in for _ in range(jax.lax.axis_size(row_axis))])
+    item_now = jax.lax.all_to_all(reply, row_axis, 0, 0)
+    return jnp.concatenate(item_now, 1)
 
 
 def for_sending(array):
@@ -206,10 +212,7 @@
     key_rows = keys.reshape(tok_rows, head_count, head_width)
     value_rows = values.reshape(tok_rows, head_count, head_width)
     grad_out = jnp.einsum(
-        "td,fd->tf",
-        lax.all_gather(out_grad, "tp", axis=1, tiled=True),
-        w_out,
-        preferred_element_type=jnp.float32,
+        "td,fd->tf", members_all_render(out_grad, "tp"), w_out, preferred_element_type=jnp.float32
     )
     grad_rows = grad_out.astype(jnp.bfloat16).reshape(tok_rows, head_count, head_width)
     level_data = []

time: 902 us -> 893 us (0.990)
  between operations: 15.9 us -> 2.89 us
  loops' own time: 5.49 us -> 16.5 us
    all_gather x1 -> x0, waiting for transfers between devices: 21.8 us -> none  [local(): lax.all_gather(out_grad, 'tp', axis=1, tiled=True)]
    all_to_all x0 -> x1, waiting for transfers between devices: none -> 15.7 us  [members_all_render(): item_now = jax.lax.all_to_all(reply, row_axis, 0, 0)]
    another operation x3, loops' own time: 2.6 us -> 13.6 us  [forward_relay(): lax.fori_loop(1, relay_turns + 1, forward_turn_body, (key_pair, running,...]
    ppermute x156, waiting for transfers between devices: 601 us -> 611 us  [passed_along(): return lax.ppermute(block, axis, route)]
  transfers between devices with their start and end apart: 157 -> 157, of which waited for: 144 -> 144; matrix products, arithmetic and copies ran while one was open for 13% -> 12% of each run, Pallas kernels for 0% -> 0%
where the time goes in v1:
time: 893 us; the launch traced here: 884 us
  waiting for transfers between devices  626 us (70%)
  matrix products  109 us (12%)
  local copies, waits for them, and re-layouts  52.4 us (6%)
  other arithmetic  49 us (5%)
  starting transfers between devices  27.4 us (3%)
  loops' own time  16.5 us (2%)
    ppermute x156, waiting for transfers between devices, passed_along(): return lax.ppermute(block, axis, route)  611 us
    ppermute x156, starting transfers between devices, passed_along(): return lax.ppermute(block, axis, route)  20.7 us
    dot_general x28, matrix products, forward_tile(): jnp.einsum('hab,bhd->ahd', weights_high, key_pair[1], preferred_element_t...  18.2 us
  transfers between devices with their start and end apart: 157, of which 144 were waited for; matrix products, arithmetic and copies ran while one was open for 12% of the time, Pallas kernels for 0%

profile of v1, /device:TPU:8, one launch (start us, length us, event | category | flops | bytes accessed | tf_op | source)
XLA Modules:
  0.0 883.6 jit_solution(608756024212365701)
XLA Ops:
  18.5 15.7 %all-to-all-done = bf16[4,256,1024]{1,2,0:T(8,128)(2,1)} async-done(((bf16[4,256,1024]{1,2,0:T(8,128)(2,1)}), bf16[4,256,1024]{1,2,0:T(8,128)(2,1)}, u32[]{:S(2)}, u32[]{:S(2)}) %all-to-all-start) | async-done | bytes 2097184 | tf_op jit(solution)/shard_map/all_to_all | solution.py:15
  60.9 70.5 %while.144 = (s32[]{:T(128)}, bf16[256,4,128]{2,0,1:T(8,128)(2,1)}, bf16[256,4,128]{2,0,1:T(8,128)(2,1)}, f32[256,4]{0,1:T(4,128)S(1)}, f32[256,4]{0,1:T(4,128)S...) while((s32[]{:T(128)}, bf16[256,4,128]{2,0,1:T(8,128)(2,1)}, ...), condition=%wide.region_5.6_spmd, body=%wide.region_2.5_spmd.sunk | while | flops 208857616 | bytes 10641786 | solution.py:127
  63.8 12.9 %collective-permute-done = bf16[256,4,128]{2,0,1:T(8,128)(2,1)S(1)} collective-permute-done((bf16[256,4,128]{2,0,1:T(8,128)(2,1)}, bf16[256,4,128]{2,0,1:T(8,128)(2,1)S(1)}, u32[]{:S(2)}, u32[]{:S(2)}) %collective-permute-start) | collective-permute-done | bytes 262176 | tf_op jit(solution)/shard_map/while/body/eval_jaxpr/ppermute | solution.py:30
  86.6 14.3 %collective-permute-done = bf16[256,4,128]{2,0,1:T(8,128)(2,1)S(1)} collective-permute-done((bf16[256,4,128]{2,0,1:T(8,128)(2,1)}, bf16[256,4,128]{2,0,1:T(8,128)(2,1)S(1)}, u32[]{:S(2)}, u32[]{:S(2)}) %collective-permute-start) | collective-permute-done | bytes 262176 | tf_op jit(solution)/shard_map/while/body/eval_jaxpr/ppermute | solution.py:30
  110.0 14.3 %collective-permute-done = bf16[256,4,128]{2,0,1:T(8,128)(2,1)S(1)} collective-permute-done((bf16[256,4,128]{2,0,1:T(8,128)(2,1)}, bf16[256,4,128]{2,0,1:T(8,128)(2,1)S(1)}, u32[]{:S(2)}, u32[]{:S(2)}) %collective-permute-start) | collective-permute-done | bytes 262176 | tf_op jit(solution)/shard_map/while/body/eval_jaxpr/ppermute | solution.py:30
  132.1 185.1 %while.146 = (s32[]{:T(128)}, bf16[64,4,128]{2,0,1:T(8,128)(2,1)S(1)}, bf16[64,4,128]{2,0,1:T(8,128)(2,1)S(1)}, f32[64,4]{0,1:T(4,128)S(1)}, f32[64,4]{0,1:T(4,1...) while((s32[]{:T(128)}, ...), condition=%wide.region_23.24_spmd, body=%wide.region_20.23_spmd.sunk | while | flops 13138703 | bytes 1874298 | solution.py:127
  143.7 9.8 %collective-permute-done.4 = bf16[64,4,128]{2,0,1:T(8,128)(2,1)S(1)} collective-permute-done((bf16[64,4,128]{2,0,1:T(8,128)(2,1)S(1)}, bf16[64,4,128]{2,0,1:T(8,128)(2,1)S(1)}, u32[]{:S(2)}, u32[]{:S(2)}) %collective-permute-start.4) | collective-permute-done | bytes 65568 | tf_op jit(solution)/shard_map/while/body/eval_jaxpr/ppermute | solution.py:30
  155.1 9.8 %collective-permute-done.4 = bf16[64,4,128]{2,0,1:T(8,128)(2,1)S(1)} collective-permute-done((bf16[64,4,128]{2,0,1:T(8,128)(2,1)S(1)}, bf16[64,4,128]{2,0,1:T(8,128)(2,1)S(1)}, u32[]{:S(2)}, u32[]{:S(2)}) %collective-permute-start.4) | collective-permute-done | bytes 65568 | tf_op jit(solution)/shard_map/while/body/eval_jaxpr/ppermute | solution.py:30
  166.6 9.8 %collective-permute-done.4 = bf16[64,4,128]{2,0,1:T(8,128)(2,1)S(1)} collective-permute-done((bf16[64,4,128]{2,0,1:T(8,128)(2,1)S(1)}, bf16[64,4,128]{2,0,1:T(8,128)(2,1)S(1)}, u32[]{:S(2)}, u32[]{:S(2)}) %collective-permute-start.4) | collective-permute-done | bytes 65568 | tf_op jit(solution)/shard_map/while/body/eval_jaxpr/ppermute | solution.py:30
  178.0 9.8 %collective-permute-done.4 = bf16[64,4,128]{2,0,1:T(8,128)(2,1)S(1)} collective-permute-done((bf16[64,4,128]{2,0,1:T(8,128)(2,1)S(1)}, bf16[64,4,128]{2,0,1:T(8,128)(2,1)S(1)}, u32[]{:S(2)}, u32[]{:S(2)}) %collective-permute-start.4) | collective-permute-done | bytes 65568 | tf_op jit(solution)/shard_map/while/body/eval_jaxpr/ppermute | solution.py:30
  189.5 9.8 %collective-permute-done.4 = bf16[64,4,128]{2,0,1:T(8,128)(2,1)S(1)} collective-permute-done((bf16[64,4,128]{2,0,1:T(8,128)(2,1)S(1)}, bf16[64,4,128]{2,0,1:T(8,128)(2,1)S(1)}, u32[]{:S(2)}, u32[]{:S(2)}) %collective-permute-start.4) | collective-permute-done | bytes 65568 | tf_op jit(solution)/shard_map/while/body/eval_jaxpr/ppermute | solution.py:30
  200.9 9.8 %collective-permute-done.4 = bf16[64,4,128]{2,0,1:T(8,128)(2,1)S(1)} collective-permute-done((bf16[64,4,128]{2,0,1:T(8,128)(2,1)S(1)}, bf16[64,4,128]{2,0,1:T(8,128)(2,1)S(1)}, u32[]{:S(2)}, u32[]{:S(2)}) %collective-permute-start.4) | collective-permute-done | bytes 65568 | tf_op jit(solution)/shard_map/while/body/eval_jaxpr/ppermute | solution.py:30
  212.7 10.5 %collective-permute-done.4 = bf16[64,4,128]{2,0,1:T(8,128)(2,1)S(1)} collective-permute-done((bf16[64,4,128]{2,0,1:T(8,128)(2,1)S(1)}, bf16[64,4,128]{2,0,1:T(8,128)(2,1)S(1)}, u32[]{:S(2)}, u32[]{:S(2)}) %collective-permute-start.4) | collective-permute-done | bytes 65568 | tf_op jit(solution)/shard_map/while/body/eval_jaxpr/ppermute | solution.py:30
  225.5 10.3 %collective-permute-done.4 = bf16[64,4,128]{2,0,1:T(8,128)(2,1)S(1)} collective-permute-done((bf16[64,4,128]{2,0,1:T(8,128)(2,1)S(1)}, bf16[64,4,128]{2,0,1:T(8,128)(2,1)S(1)}, u32[]{:S(2)}, u32[]{:S(2)}) %collective-permute-start.4) | collective-permute-done | bytes 65568 | tf_op jit(solution)/shard_map/while/body/eval_jaxpr/ppermute | solution.py:30
  237.4 9.8 %collective-permute-done.4 = bf16[64,4,128]{2,0,1:T(8,128)(2,1)S(1)} collective-permute-done((bf16[64,4,128]{2,0,1:T(8,128)(2,1)S(1)}, bf16[64,4,128]{2,0,1:T(8,128)(2,1)S(1)}, u32[]{:S(2)}, u32[]{:S(2)}) %collective-permute-start.4) | collective-permute-done | bytes 65568 | tf_op jit(solution)/shard_map/while/body/eval_jaxpr/ppermute | solution.py:30
  248.9 9.8 %collective-permute-done.4 = bf16[64,4,128]{2,0,1:T(8,128)(2,1)S(1)} collective-permute-done((bf16[64,4,128]{2,0,1:T(8,128)(2,1)S(1)}, bf16[64,4,128]{2,0,1:T(8,128)(2,1)S(1)}, u32[]{:S(2)}, u32[]{:S(2)}) %collective-permute-start.4) | collective-permute-done | bytes 65568 | tf_op jit(solution)/shard_map/while/body/eval_jaxpr/ppermute | solution.py:30
  260.3 9.8 %collective-permute-done.4 = bf16[64,4,128]{2,0,1:T(8,128)(2,1)S(1)} collective-permute-done((bf16[64,4,128]{2,0,1:T(8,128)(2,1)S(1)}, bf16[64,4,128]{2,0,1:T(8,128)(2,1)S(1)}, u32[]{:S(2)}, u32[]{:S(2)}) %collective-permute-start.4) | collective-permute-done | bytes 65568 | tf_op jit(solution)/shard_map/while/body/eval_jaxpr/ppermute | solution.py:30
  271.8 9.8 %collective-permute-done.4 = bf16[64,4,128]{2,0,1:T(8,128)(2,1)S(1)} collective-permute-done((bf16[64,4,128]{2,0,1:T(8,128)(2,1)S(1)}, bf16[64,4,128]{2,0,1:T(8,128)(2,1)S(1)}, u32[]{:S(2)}, u32[]{:S(2)}) %collective-permute-start.4) | collective-permute-done | bytes 65568 | tf_op jit(solution)/shard_map/while/body/eval_jaxpr/ppermute | solution.py:30
  283.2 9.8 %collective-permute-done.4 = bf16[64,4,128]{2,0,1:T(8,128)(2,1)S(1)} collective-permute-done((bf16[64,4,128]{2,0,1:T(8,128)(2,1)S(1)}, bf16[64,4,128]{2,0,1:T(8,128)(2,1)S(1)}, u32[]{:S(2)}, u32[]{:S(2)}) %collective-permute-start.4) | collective-permute-done | bytes 65568 | tf_op jit(solution)/shard_map/while/body/eval_jaxpr/ppermute | solution.py:30
  294.7 9.8 %collective-permute-done.4 = bf16[64,4,128]{2,0,1:T(8,128)(2,1)S(1)} collective-permute-done((bf16[64,4,128]{2,0,1:T(8,128)(2,1)S(1)}, bf16[64,4,128]{2,0,1:T(8,128)(2,1)S(1)}, u32[]{:S(2)}, u32[]{:S(2)}) %collective-permute-start.4) | collective-permute-done | bytes 65568 | tf_op jit(solution)/shard_map/while/body/eval_jaxpr/ppermute | solution.py:30
  306.1 9.8 %collective-permute-done.4 = bf16[64,4,128]{2,0,1:T(8,128)(2,1)S(1)} collective-permute-done((bf16[64,4,128]{2,0,1:T(8,128)(2,1)S(1)}, bf16[64,4,128]{2,0,1:T(8,128)(2,1)S(1)}, u32[]{:S(2)}, u32[]{:S(2)}) %collective-permute-start.4) | collective-permute-done | bytes 65568 | tf_op jit(solution)/shard_map/while/body/eval_jaxpr/ppermute | solution.py:30
  320.3 99.2 %while.145 = (s32[]{:T(128)}, bf16[128,4,128]{2,0,1:T(8,128)(2,1)S(1)}, bf16[128,4,128]{2,0,1:T(8,128)(2,1)S(1)}, f32[128,4]{0,1:T(4,128)S(1)}, f32[128,4]{0,1:T...) while((s32[]{:T(128)}, ...), condition=%wide.region_14.15_spmd, body=%wide.region_11.14_spmd.sunk | while | flops 52327952 | bytes 4272506 | solution.py:127
  321.2 9.9 %collective-permute-done.2 = bf16[128,4,128]{2,0,1:T(8,128)(2,1)S(1)} collective-permute-done((bf16[128,4,128]{2,0,1:T(8,128)(2,1)S(1)}, bf16[128,4,128]{2,0,1:T(8,128)(2,1)S(1)}, u32[]{:S(2)}, u32[]{:S(2)}) %collective-permute-start.2) | collective-permute-done | bytes 131104 | tf_op jit(solution)/shard_map/while/body/eval_jaxpr/ppermute | solution.py:30
  335.3 9.9 %collective-permute-done.2 = bf16[128,4,128]{2,0,1:T(8,128)(2,1)S(1)} collective-permute-done((bf16[128,4,128]{2,0,1:T(8,128)(2,1)S(1)}, bf16[128,4,128]{2,0,1:T(8,128)(2,1)S(1)}, u32[]{:S(2)}, u32[]{:S(2)}) %collective-permute-start.2) | collective-permute-done | bytes 131104 | tf_op jit(solution)/shard_map/while/body/eval_jaxpr/ppermute | solution.py:30
  349.4 9.9 %collective-permute-done.2 = bf16[128,4,128]{2,0,1:T(8,128)(2,1)S(1)} collective-permute-done((bf16[128,4,128]{2,0,1:T(8,128)(2,1)S(1)}, bf16[128,4,128]{2,0,1:T(8,128)(2,1)S(1)}, u32[]{:S(2)}, u32[]{:S(2)}) %collective-permute-start.2) | collective-permute-done | bytes 131104 | tf_op jit(solution)/shard_map/while/body/eval_jaxpr/ppermute | solution.py:30
  363.5 9.9 %collective-permute-done.2 = bf16[128,4,128]{2,0,1:T(8,128)(2,1)S(1)} collective-permute-done((bf16[128,4,128]{2,0,1:T(8,128)(2,1)S(1)}, bf16[128,4,128]{2,0,1:T(8,128)(2,1)S(1)}, u32[]{:S(2)}, u32[]{:S(2)}) %collective-permute-start.2) | collective-permute-done | bytes 131104 | tf_op jit(solution)/shard_map/while/body/eval_jaxpr/ppermute | solution.py:30
  377.6 9.9 %collective-permute-done.2 = bf16[128,4,128]{2,0,1:T(8,128)(2,1)S(1)} collective-permute-done((bf16[128,4,128]{2,0,1:T(8,128)(2,1)S(1)}, bf16[128,4,128]{2,0,1:T(8,128)(2,1)S(1)}, u32[]{:S(2)}, u32[]{:S(2)}) %collective-permute-start.2) | collective-permute-done | bytes 131104 | tf_op jit(solution)/shard_map/while/body/eval_jaxpr/ppermute | solution.py:30
  392.3 9.9 %collective-permute-done.2 = bf16[128,4,128]{2,0,1:T(8,128)(2,1)S(1)} collective-permute-done((bf16[128,4,128]{2,0,1:T(8,128)(2,1)S(1)}, bf16[128,4,128]{2,0,1:T(8,128)(2,1)S(1)}, u32[]{:S(2)}, u32[]{:S(2)}) %collective-permute-start.2) | collective-permute-done | bytes 131104 | tf_op jit(solution)/shard_map/while/body/eval_jaxpr/ppermute | solution.py:30
  406.4 9.9 %collective-permute-done.2 = bf16[128,4,128]{2,0,1:T(8,128)(2,1)S(1)} collective-permute-done((bf16[128,4,128]{2,0,1:T(8,128)(2,1)S(1)}, bf16[128,4,128]{2,0,1:T(8,128)(2,1)S(1)}, u32[]{:S(2)}, u32[]{:S(2)}) %collective-permute-start.2) | collective-permute-done | bytes 131104 | tf_op jit(solution)/shard_map/while/body/eval_jaxpr/ppermute | solution.py:30
  451.1 74.7 %while.147 = (s32[]{:T(128)}, bf16[256,4,128]{2,0,1:T(8,128)(2,1)S(1)}, bf16[256,4,128]{2,0,1:T(8,128)(2,1)S(1)}, bf16[256,4,128]{2,0,1:T(8,128)(2,1)}, bf16[256...) while((s32[]{:T(128)}, ...), condition=%wide.region_26.27_spmd, body=%wide.region_25.26_spmd.sunk | while | flops 339403264 | bytes 13939170 | solution.py:188
  452.2 13.9 %collective-permute-done.6 = bf16[256,4,128]{2,0,1:T(8,128)(2,1)S(1)} collective-permute-done((bf16[256,4,128]{2,0,1:T(8,128)(2,1)S(1)}, bf16[256,4,128]{2,0,1:T(8,128)(2,1)S(1)}, u32[]{:S(2)}, u32[]{:S(2)}) %collective-permute-start.6) | collective-permute-done | bytes 262176 | tf_op jit(solution)/shard_map/while/body/eval_jaxpr/ppermute | solution.py:30
  478.2 14.1 %collective-permute-done.6 = bf16[256,4,128]{2,0,1:T(8,128)(2,1)S(1)} collective-permute-done((bf16[256,4,128]{2,0,1:T(8,128)(2,1)S(1)}, bf16[256,4,128]{2,0,1:T(8,128)(2,1)S(1)}, u32[]{:S(2)}, u32[]{:S(2)}) %collective-permute-start.6) | collective-permute-done | bytes 262176 | tf_op jit(solution)/shard_map/while/body/eval_jaxpr/ppermute | solution.py:30
  503.4 11.5 %collective-permute-done.6 = bf16[256,4,128]{2,0,1:T(8,128)(2,1)S(1)} collective-permute-done((bf16[256,4,128]{2,0,1:T(8,128)(2,1)S(1)}, bf16[256,4,128]{2,0,1:T(8,128)(2,1)S(1)}, u32[]{:S(2)}, u32[]{:S(2)}) %collective-permute-start.6) | collective-permute-done | bytes 262176 | tf_op jit(solution)/shard_map/while/body/eval_jaxpr/ppermute | solution.py:30
  528.1 134.4 %while.148 = (s32[]{:T(128)}, bf16[128,4,128]{2,0,1:T(8,128)(2,1)}, bf16[128,4,128]{2,0,1:T(8,128)(2,1)S(1)}, bf16[128,4,128]{2,0,1:T(8,128)(2,1)}, bf16[128,4,1...) while((s32[]{:T(128)}, bf16[128,4,128]{2,0,1:T(8,128)(2,1)}, ...), condition=%wide.region_31.32_spmd, body=%wide.region_30.31_spmd.sunk | while | flops 85094928 | bytes 5790178 | solution.py:188
  550.6 11.4 %collective-permute-done.10 = bf16[128,4,128]{2,0,1:T(8,128)(2,1)S(1)} collective-permute-done((bf16[128,4,128]{2,0,1:T(8,128)(2,1)}, bf16[128,4,128]{2,0,1:T(8,128)(2,1)S(1)}, u32[]{:S(2)}, u32[]{:S(2)}) %collective-permute-start.10) | collective-permute-done | bytes 131104 | tf_op jit(solution)/shard_map/while/body/eval_jaxpr/ppermute | solution.py:30
  571.4 11.5 %collective-permute-done.10 = bf16[128,4,128]{2,0,1:T(8,128)(2,1)S(1)} collective-permute-done((bf16[128,4,128]{2,0,1:T(8,128)(2,1)}, bf16[128,4,128]{2,0,1:T(8,128)(2,1)S(1)}, u32[]{:S(2)}, u32[]{:S(2)}) %collective-permute-start.10) | collective-permute-done | bytes 131104 | tf_op jit(solution)/shard_map/while/body/eval_jaxpr/ppermute | solution.py:30
  591.4 11.5 %collective-permute-done.10 = bf16[128,4,128]{2,0,1:T(8,128)(2,1)S(1)} collective-permute-done((bf16[128,4,128]{2,0,1:T(8,128)(2,1)}, bf16[128,4,128]{2,0,1:T(8,128)(2,1)S(1)}, u32[]{:S(2)}, u32[]{:S(2)}) %collective-permute-start.10) | collective-permute-done | bytes 131104 | tf_op jit(solution)/shard_map/while/body/eval_jaxpr/ppermute | solution.py:30
  610.4 11.5 %collective-permute-done.10 = bf16[128,4,128]{2,0,1:T(8,128)(2,1)S(1)} collective-permute-done((bf16[128,4,128]{2,0,1:T(8,128)(2,1)}, bf16[128,4,128]{2,0,1:T(8,128)(2,1)S(1)}, u32[]{:S(2)}, u32[]{:S(2)}) %collective-permute-start.10) | collective-permute-done | bytes 131104 | tf_op jit(solution)/shard_map/while/body/eval_jaxpr/ppermute | solution.py:30
  628.5 10.1 %collective-permute-done.10 = bf16[128,4,128]{2,0,1:T(8,128)(2,1)S(1)} collective-permute-done((bf16[128,4,128]{2,0,1:T(8,128)(2,1)}, bf16[128,4,128]{2,0,1:T(8,128)(2,1)S(1)}, u32[]{:S(2)}, u32[]{:S(2)}) %collective-permute-start.10) | collective-permute-done | bytes 131104 | tf_op jit(solution)/shard_map/while/body/eval_jaxpr/ppermute | solution.py:30
  644.5 10.1 %collective-permute-done.10 = bf16[128,4,128]{2,0,1:T(8,128)(2,1)S(1)} collective-permute-done((bf16[128,4,128]{2,0,1:T(8,128)(2,1)}, bf16[128,4,128]{2,0,1:T(8,128)(2,1)S(1)}, u32[]{:S(2)}, u32[]{:S(2)}) %collective-permute-start.10) | collective-permute-done | bytes 131104 | tf_op jit(solution)/shard_map/while/body/eval_jaxpr/ppermute | solution.py:30
  662.6 194.8 %while.149 = (s32[]{:T(128)}, bf16[64,4,128]{2,0,1:T(8,128)(2,1)S(1)}, bf16[64,4,128]{2,0,1:T(8,128)(2,1)S(1)}, bf16[64,4,128]{2,0,1:T(8,128)(2,1)S(1)}, bf16[64...) while((s32[]{:T(128)}, ...), condition=%wide.region_36.37_spmd, body=%wide.region_35.36_spmd.sunk | while | flops 21395728 | bytes 2600418 | solution.py:188
  663.1 10.0 %collective-permute-done.14 = bf16[64,4,128]{2,0,1:T(8,128)(2,1)S(1)} collective-permute-done((bf16[64,4,128]{2,0,1:T(8,128)(2,1)S(1)}, bf16[64,4,128]{2,0,1:T(8,128)(2,1)S(1)}, u32[]{:S(2)}, u32[]{:S(2)}) %collective-permute-start.14) | collective-permute-done | bytes 65568 | tf_op jit(solution)/shard_map/while/body/eval_jaxpr/ppermute | solution.py:30
  675.9 9.6 %collective-permute-done.14 = bf16[64,4,128]{2,0,1:T(8,128)(2,1)S(1)} collective-permute-done((bf16[64,4,128]{2,0,1:T(8,128)(2,1)S(1)}, bf16[64,4,128]{2,0,1:T(8,128)(2,1)S(1)}, u32[]{:S(2)}, u32[]{:S(2)}) %collective-permute-start.14) | collective-permute-done | bytes 65568 | tf_op jit(solution)/shard_map/while/body/eval_jaxpr/ppermute | solution.py:30
  688.3 9.6 %collective-permute-done.14 = bf16[64,4,128]{2,0,1:T(8,128)(2,1)S(1)} collective-permute-done((bf16[64,4,128]{2,0,1:T(8,128)(2,1)S(1)}, bf16[64,4,128]{2,0,1:T(8,128)(2,1)S(1)}, u32[]{:S(2)}, u32[]{:S(2)}) %collective-permute-start.14) | collective-permute-done | bytes 65568 | tf_op jit(solution)/shard_map/while/body/eval_jaxpr/ppermute | solution.py:30
  713.1 9.6 %collective-permute-done.14 = bf16[64,4,128]{2,0,1:T(8,128)(2,1)S(1)} collective-permute-done((bf16[64,4,128]{2,0,1:T(8,128)(2,1)S(1)}, bf16[64,4,128]{2,0,1:T(8,128)(2,1)S(1)}, u32[]{:S(2)}, u32[]{:S(2)}) %collective-permute-start.14) | collective-permute-done | bytes 65568 | tf_op jit(solution)/shard_map/while/body/eval_jaxpr/ppermute | solution.py:30
  764.9 10.3 %collective-permute-done.14 = bf16[64,4,128]{2,0,1:T(8,128)(2,1)S(1)} collective-permute-done((bf16[64,4,128]{2,0,1:T(8,128)(2,1)S(1)}, bf16[64,4,128]{2,0,1:T(8,128)(2,1)S(1)}, u32[]{:S(2)}, u32[]{:S(2)}) %collective-permute-start.14) | collective-permute-done | bytes 65568 | tf_op jit(solution)/shard_map/while/body/eval_jaxpr/ppermute | solution.py:30
  780.1 10.3 %collective-permute-done.14 = bf16[64,4,128]{2,0,1:T(8,128)(2,1)S(1)} collective-permute-done((bf16[64,4,128]{2,0,1:T(8,128)(2,1)S(1)}, bf16[64,4,128]{2,0,1:T(8,128)(2,1)S(1)}, u32[]{:S(2)}, u32[]{:S(2)}) %collective-permute-start.14) | collective-permute-done | bytes 65568 | tf_op jit(solution)/shard_map/while/body/eval_jaxpr/ppermute | solution.py:30
  794.5 10.3 %collective-permute-done.14 = bf16[64,4,128]{2,0,1:T(8,128)(2,1)S(1)} collective-permute-done((bf16[64,4,128]{2,0,1:T(8,128)(2,1)S(1)}, bf16[64,4,128]{2,0,1:T(8,128)(2,1)S(1)}, u32[]{:S(2)}, u32[]{:S(2)}) %collective-permute-start.14) | collective-permute-done | bytes 65568 | tf_op jit(solution)/shard_map/while/body/eval_jaxpr/ppermute | solution.py:30
  (1201 shorter events, 415.3 us)
Async XLA Ops:
  3.4 30.9 %all-to-all-start = ((bf16[4,256,1024]{1,2,0:T(8,128)(2,1)}), bf16[4,256,1024]{1,2,0:T(8,128)(2,1)}, u32[]{:S(2)}, u32[]{:S(2)}) async-start(bf16[4,256,1024]{1,2,0:T(8,128)(2,1)} %stack.2), calls=%async_computation | async-start | bytes 4194304 | tf_op jit(solution)/shard_map/all_to_all | solution.py:15
  60.9 15.8 %collective-permute-start = (bf16[256,4,128]{2,0,1:T(8,128)(2,1)}, bf16[256,4,128]{2,0,1:T(8,128)(2,1)S(1)}, u32[]{:S(2)}, u32[]{:S(2)}) collective-permute-start(bf16[256,4,128]{2,0,1:T(8,128)(2,1)} %get-tuple-element.3054), channel_id=1, source_target_pairs={{252,0},{0,4},{4,8},{8,12},{12,16},{16,20},{20,24},{24,28},{28,32}... | collective-permute-start | bytes 786440 | tf_op jit(solution)/shard_map/while/body/eval_jaxpr/ppermute | solution.py:30
  61.2 20.4 %collective-permute-start.1 = (bf16[256,4,128]{2,0,1:T(8,128)(2,1)}, bf16[256,4,128]{2,0,1:T(8,128)(2,1)S(1)}, u32[]{:S(2)}, u32[]{:S(2)}) collective-permute-start(bf16[256,4,128]{2,0,1:T(8,128)(2,1)} %get-tuple-element.3055), channel_id=1, source_target_pairs={{252,0},{0,4},{4,8},{8,12},{12,16},{16,20},{20,24},{24,28},{28,32}... | collective-permute-start | bytes 786440 | tf_op jit(solution)/shard_map/while/body/eval_jaxpr/ppermute | solution.py:30
  85.7 15.3 %collective-permute-start = (bf16[256,4,128]{2,0,1:T(8,128)(2,1)}, bf16[256,4,128]{2,0,1:T(8,128)(2,1)S(1)}, u32[]{:S(2)}, u32[]{:S(2)}) collective-permute-start(bf16[256,4,128]{2,0,1:T(8,128)(2,1)} %get-tuple-element.3054), channel_id=1, source_target_pairs={{252,0},{0,4},{4,8},{8,12},{12,16},{16,20},{20,24},{24,28},{28,32}... | collective-permute-start | bytes 786440 | tf_op jit(solution)/shard_map/while/body/eval_jaxpr/ppermute | solution.py:30
  85.8 19.1 %collective-permute-start.1 = (bf16[256,4,128]{2,0,1:T(8,128)(2,1)}, bf16[256,4,128]{2,0,1:T(8,128)(2,1)S(1)}, u32[]{:S(2)}, u32[]{:S(2)}) collective-permute-start(bf16[256,4,128]{2,0,1:T(8,128)(2,1)} %get-tuple-element.3055), channel_id=1, source_target_pairs={{252,0},{0,4},{4,8},{8,12},{12,16},{16,20},{20,24},{24,28},{28,32}... | collective-permute-start | bytes 786440 | tf_op jit(solution)/shard_map/while/body/eval_jaxpr/ppermute | solution.py:30
  109.0 15.3 %collective-permute-start = (bf16[256,4,128]{2,0,1:T(8,128)(2,1)}, bf16[256,4,128]{2,0,1:T(8,128)(2,1)S(1)}, u32[]{:S(2)}, u32[]{:S(2)}) collective-permute-start(bf16[256,4,128]{2,0,1:T(8,128)(2,1)} %get-tuple-element.3054), channel_id=1, source_target_pairs={{252,0},{0,4},{4,8},{8,12},{12,16},{16,20},{20,24},{24,28},{28,32}... | collective-permute-start | bytes 786440 | tf_op jit(solution)/shard_map/while/body/eval_jaxpr/ppermute | solution.py:30
  109.1 18.2 %collective-permute-start.1 = (bf16[256,4,128]{2,0,1:T(8,128)(2,1)}, bf16[256,4,128]{2,0,1:T(8,128)(2,1)S(1)}, u32[]{:S(2)}, u32[]{:S(2)}) collective-permute-start(bf16[256,4,128]{2,0,1:T(8,128)(2,1)} %get-tuple-element.3055), channel_id=1, source_target_pairs={{252,0},{0,4},{4,8},{8,12},{12,16},{16,20},{20,24},{24,28},{28,32}... | collective-permute-start | bytes 786440 | tf_op jit(solution)/shard_map/while/body/eval_jaxpr/ppermute | solution.py:30
  376.8 13.2 %collective-permute-start.3 = (bf16[128,4,128]{2,0,1:T(8,128)(2,1)S(1)}, bf16[128,4,128]{2,0,1:T(8,128)(2,1)S(1)}, u32[]{:S(2)}, u32[]{:S(2)}) collective-permute-start(bf16[128,4,128]{2,0,1:T(8,128)(2,1)S(1)} %get-tuple-element.2965), channel_id=1, source_target_pairs={{252,0},{0,4},{4,8},{8,12},{12,16},{16,20},{20,24},{24,28},{28,32}... | collective-permute-start | bytes 393224 | tf_op jit(solution)/shard_map/while/body/eval_jaxpr/ppermute | solution.py:30
  451.1 15.0 %collective-permute-start.6 = (bf16[256,4,128]{2,0,1:T(8,128)(2,1)S(1)}, bf16[256,4,128]{2,0,1:T(8,128)(2,1)S(1)}, u32[]{:S(2)}, u32[]{:S(2)}) collective-permute-start(bf16[256,4,128]{2,0,1:T(8,128)(2,1)S(1)} %get-tuple-element.3156), channel_id=1, source_target_pairs={{252,0},{0,4},{4,8},{8,12},{12,16},{16,20},{20,24},{24,28},{28,32}... | collective-permute-start | bytes 786440 | tf_op jit(solution)/shard_map/while/body/eval_jaxpr/ppermute | solution.py:30
  451.2 19.5 %collective-permute-start.7 = (bf16[256,4,128]{2,0,1:T(8,128)(2,1)S(1)}, bf16[256,4,128]{2,0,1:T(8,128)(2,1)S(1)}, u32[]{:S(2)}, u32[]{:S(2)}) collective-permute-start(bf16[256,4,128]{2,0,1:T(8,128)(2,1)S(1)} %get-tuple-element.3157), channel_id=1, source_target_pairs={{252,0},{0,4},{4,8},{8,12},{12,16},{16,20},{20,24},{24,28},{28,32}... | collective-permute-start | bytes 786440 | tf_op jit(solution)/shard_map/while/body/eval_jaxpr/ppermute | solution.py:30
  451.3 22.2 %collective-permute-start.8 = (bf16[256,4,128]{2,0,1:T(8,128)(2,1)}, bf16[256,4,128]{2,0,1:T(8,128)(2,1)S(1)}, u32[]{:S(2)}, u32[]{:S(2)}) collective-permute-start(bf16[256,4,128]{2,0,1:T(8,128)(2,1)} %get-tuple-element.3158), channel_id=1, source_target_pairs={{252,0},{0,4},{4,8},{8,12},{12,16},{16,20},{20,24},{24,28},{28,32}... | collective-permute-start | bytes 786440 | tf_op jit(solution)/shard_map/while/body/eval_jaxpr/ppermute | solution.py:30
  451.4 24.9 %collective-permute-start.9 = (bf16[256,4,128]{2,0,1:T(8,128)(2,1)}, bf16[256,4,128]{2,0,1:T(8,128)(2,1)S(1)}, u32[]{:S(2)}, u32[]{:S(2)}) collective-permute-start(bf16[256,4,128]{2,0,1:T(8,128)(2,1)} %get-tuple-element.3159), channel_id=1, source_target_pairs={{252,0},{0,4},{4,8},{8,12},{12,16},{16,20},{20,24},{24,28},{28,32}... | collective-permute-start | bytes 786440 | tf_op jit(solution)/shard_map/while/body/eval_jaxpr/ppermute | solution.py:30
  477.3 15.0 %collective-permute-start.6 = (bf16[256,4,128]{2,0,1:T(8,128)(2,1)S(1)}, bf16[256,4,128]{2,0,1:T(8,128)(2,1)S(1)}, u32[]{:S(2)}, u32[]{:S(2)}) collective-permute-start(bf16[256,4,128]{2,0,1:T(8,128)(2,1)S(1)} %get-tuple-element.3156), channel_id=1, source_target_pairs={{252,0},{0,4},{4,8},{8,12},{12,16},{16,20},{20,24},{24,28},{28,32}... | collective-permute-start | bytes 786440 | tf_op jit(solution)/shard_map/while/body/eval_jaxpr/ppermute | solution.py:30
  477.3 18.5 %collective-permute-start.7 = (bf16[256,4,128]{2,0,1:T(8,128)(2,1)S(1)}, bf16[256,4,128]{2,0,1:T(8,128)(2,1)S(1)}, u32[]{:S(2)}, u32[]{:S(2)}) collective-permute-start(bf16[256,4,128]{2,0,1:T(8,128)(2,1)S(1)} %get-tuple-element.3157), channel_id=1, source_target_pairs={{252,0},{0,4},{4,8},{8,12},{12,16},{16,20},{20,24},{24,28},{28,32}... | collective-permute-start | bytes 786440 | tf_op jit(solution)/shard_map/while/body/eval_jaxpr/ppermute | solution.py:30
  477.3 21.3 %collective-permute-start.8 = (bf16[256,4,128]{2,0,1:T(8,128)(2,1)}, bf16[256,4,128]{2,0,1:T(8,128)(2,1)S(1)}, u32[]{:S(2)}, u32[]{:S(2)}) collective-permute-start(bf16[256,4,128]{2,0,1:T(8,128)(2,1)} %get-tuple-element.3158), channel_id=1, source_target_pairs={{252,0},{0,4},{4,8},{8,12},{12,16},{16,20},{20,24},{24,28},{28,32}... | collective-permute-start | bytes 786440 | tf_op jit(solution)/shard_map/while/body/eval_jaxpr/ppermute | solution.py:30
  477.3 24.1 %collective-permute-start.9 = (bf16[256,4,128]{2,0,1:T(8,128)(2,1)}, bf16[256,4,128]{2,0,1:T(8,128)(2,1)S(1)}, u32[]{:S(2)}, u32[]{:S(2)}) collective-permute-start(bf16[256,4,128]{2,0,1:T(8,128)(2,1)} %get-tuple-element.3159), channel_id=1, source_target_pairs={{252,0},{0,4},{4,8},{8,12},{12,16},{16,20},{20,24},{24,28},{28,32}... | collective-permute-start | bytes 786440 | tf_op jit(solution)/shard_map/while/body/eval_jaxpr/ppermute | solution.py:30
  502.5 15.1 %collective-permute-start.7 = (bf16[256,4,128]{2,0,1:T(8,128)(2,1)S(1)}, bf16[256,4,128]{2,0,1:T(8,128)(2,1)S(1)}, u32[]{:S(2)}, u32[]{:S(2)}) collective-permute-start(bf16[256,4,128]{2,0,1:T(8,128)(2,1)S(1)} %get-tuple-element.3157), channel_id=1, source_target_pairs={{252,0},{0,4},{4,8},{8,12},{12,16},{16,20},{20,24},{24,28},{28,32}... | collective-permute-start | bytes 786440 | tf_op jit(solution)/shard_map/while/body/eval_jaxpr/ppermute | solution.py:30
  502.5 17.9 %collective-permute-start.8 = (bf16[256,4,128]{2,0,1:T(8,128)(2,1)}, bf16[256,4,128]{2,0,1:T(8,128)(2,1)S(1)}, u32[]{:S(2)}, u32[]{:S(2)}) collective-permute-start(bf16[256,4,128]{2,0,1:T(8,128)(2,1)} %get-tuple-element.3158), channel_id=1, source_target_pairs={{252,0},{0,4},{4,8},{8,12},{12,16},{16,20},{20,24},{24,28},{28,32}... | collective-permute-start | bytes 786440 | tf_op jit(solution)/shard_map/while/body/eval_jaxpr/ppermute | solution.py:30
  502.5 22.2 %collective-permute-start.9 = (bf16[256,4,128]{2,0,1:T(8,128)(2,1)}, bf16[256,4,128]{2,0,1:T(8,128)(2,1)S(1)}, u32[]{:S(2)}, u32[]{:S(2)}) collective-permute-start(bf16[256,4,128]{2,0,1:T(8,128)(2,1)} %get-tuple-element.3159), channel_id=1, source_target_pairs={{252,0},{0,4},{4,8},{8,12},{12,16},{16,20},{20,24},{24,28},{28,32}... | collective-permute-start | bytes 786440 | tf_op jit(solution)/shard_map/while/body/eval_jaxpr/ppermute | solution.py:30
  526.9 350.4 %collective-permute-start.18 = (bf16[256,4,128]{0,2,1:T(8,128)(2,1)S(1)}, bf16[256,4,128]{0,2,1:T(8,128)(2,1)S(1)}, u32[]{:S(2)}, u32[]{:S(2)}) collective-permute-start(bf16[256,4,128]{0,2,1:T(8,128)(2,1)S(1)} %copy.532), channel_id=1, source_target_pairs={{12,0},{16,4},{20,8},{24,12},{28,16},{32,20},{36,24},{40,28},{44,3... | collective-permute-start | bytes 786440 | tf_op jit(solution)/shard_map/ppermute | solution.py:30
  529.1 14.2 %collective-permute-start.11 = (bf16[128,4,128]{2,0,1:T(8,128)(2,1)S(1)}, bf16[128,4,128]{2,0,1:T(8,128)(2,1)S(1)}, u32[]{:S(2)}, u32[]{:S(2)}) collective-permute-start(bf16[128,4,128]{2,0,1:T(8,128)(2,1)S(1)} %get-tuple-element.3211), channel_id=1, source_target_pairs={{252,0},{0,4},{4,8},{8,12},{12,16},{16,20},{20,24},{24,28},{28,32}... | collective-permute-start | bytes 393224 | tf_op jit(solution)/shard_map/while/body/eval_jaxpr/ppermute | solution.py:30
  531.0 15.1 %collective-permute-start.12 = (bf16[128,4,128]{2,0,1:T(8,128)(2,1)}, bf16[128,4,128]{2,0,1:T(8,128)(2,1)S(1)}, u32[]{:S(2)}, u32[]{:S(2)}) collective-permute-start(bf16[128,4,128]{2,0,1:T(8,128)(2,1)} %get-tuple-element.3212), channel_id=1, source_target_pairs={{252,0},{0,4},{4,8},{8,12},{12,16},{16,20},{20,24},{24,28},{28,32}... | collective-permute-start | bytes 393224 | tf_op jit(solution)/shard_map/while/body/eval_jaxpr/ppermute | solution.py:30
  533.3 15.6 %collective-permute-start.13 = (bf16[128,4,128]{2,0,1:T(8,128)(2,1)}, bf16[128,4,128]{2,0,1:T(8,128)(2,1)S(1)}, u32[]{:S(2)}, u32[]{:S(2)}) collective-permute-start(bf16[128,4,128]{2,0,1:T(8,128)(2,1)} %get-tuple-element.3213), channel_id=1, source_target_pairs={{252,0},{0,4},{4,8},{8,12},{12,16},{16,20},{20,24},{24,28},{28,32}... | collective-permute-start | bytes 393224 | tf_op jit(solution)/shard_map/while/body/eval_jaxpr/ppermute | solution.py:30
  549.8 15.1 %collective-permute-start.11 = (bf16[128,4,128]{2,0,1:T(8,128)(2,1)S(1)}, bf16[128,4,128]{2,0,1:T(8,128)(2,1)S(1)}, u32[]{:S(2)}, u32[]{:S(2)}) collective-permute-start(bf16[128,4,128]{2,0,1:T(8,128)(2,1)S(1)} %get-tuple-element.3211), channel_id=1, source_target_pairs={{252,0},{0,4},{4,8},{8,12},{12,16},{16,20},{20,24},{24,28},{28,32}... | collective-permute-start | bytes 393224 | tf_op jit(solution)/shard_map/while/body/eval_jaxpr/ppermute | solution.py:30
  549.8 17.9 %collective-permute-start.12 = (bf16[128,4,128]{2,0,1:T(8,128)(2,1)}, bf16[128,4,128]{2,0,1:T(8,128)(2,1)S(1)}, u32[]{:S(2)}, u32[]{:S(2)}) collective-permute-start(bf16[128,4,128]{2,0,1:T(8,128)(2,1)} %get-tuple-element.3212), channel_id=1, source_target_pairs={{252,0},{0,4},{4,8},{8,12},{12,16},{16,20},{20,24},{24,28},{28,32}... | collective-permute-start | bytes 393224 | tf_op jit(solution)/shard_map/while/body/eval_jaxpr/ppermute | solution.py:30
  549.8 19.9 %collective-permute-start.13 = (bf16[128,4,128]{2,0,1:T(8,128)(2,1)}, bf16[128,4,128]{2,0,1:T(8,128)(2,1)S(1)}, u32[]{:S(2)}, u32[]{:S(2)}) collective-permute-start(bf16[128,4,128]{2,0,1:T(8,128)(2,1)} %get-tuple-element.3213), channel_id=1, source_target_pairs={{252,0},{0,4},{4,8},{8,12},{12,16},{16,20},{20,24},{24,28},{28,32}... | collective-permute-start | bytes 393224 | tf_op jit(solution)/shard_map/while/body/eval_jaxpr/ppermute | solution.py:30
  570.6 15.2 %collective-permute-start.11 = (bf16[128,4,128]{2,0,1:T(8,128)(2,1)S(1)}, bf16[128,4,128]{2,0,1:T(8,128)(2,1)S(1)}, u32[]{:S(2)}, u32[]{:S(2)}) collective-permute-start(bf16[128,4,128]{2,0,1:T(8,128)(2,1)S(1)} %get-tuple-element.3211), channel_id=1, source_target_pairs={{252,0},{0,4},{4,8},{8,12},{12,16},{16,20},{20,24},{24,28},{28,32}... | collective-permute-start | bytes 393224 | tf_op jit(solution)/shard_map/while/body/eval_jaxpr/ppermute | solution.py:30
  570.6 17.6 %collective-permute-start.12 = (bf16[128,4,128]{2,0,1:T(8,128)(2,1)}, bf16[128,4,128]{2,0,1:T(8,128)(2,1)S(1)}, u32[]{:S(2)}, u32[]{:S(2)}) collective-permute-start(bf16[128,4,128]{2,0,1:T(8,128)(2,1)} %get-tuple-element.3212), channel_id=1, source_target_pairs={{252,0},{0,4},{4,8},{8,12},{12,16},{16,20},{20,24},{24,28},{28,32}... | collective-permute-start | bytes 393224 | tf_op jit(solution)/shard_map/while/body/eval_jaxpr/ppermute | solution.py:30
  570.6 19.0 %collective-permute-start.13 = (bf16[128,4,128]{2,0,1:T(8,128)(2,1)}, bf16[128,4,128]{2,0,1:T(8,128)(2,1)S(1)}, u32[]{:S(2)}, u32[]{:S(2)}) collective-permute-start(bf16[128,4,128]{2,0,1:T(8,128)(2,1)} %get-tuple-element.3213), channel_id=1, source_target_pairs={{252,0},{0,4},{4,8},{8,12},{12,16},{16,20},{20,24},{24,28},{28,32}... | collective-permute-start | bytes 393224 | tf_op jit(solution)/shard_map/while/body/eval_jaxpr/ppermute | solution.py:30
  590.5 15.2 %collective-permute-start.11 = (bf16[128,4,128]{2,0,1:T(8,128)(2,1)S(1)}, bf16[128,4,128]{2,0,1:T(8,128)(2,1)S(1)}, u32[]{:S(2)}, u32[]{:S(2)}) collective-permute-start(bf16[128,4,128]{2,0,1:T(8,128)(2,1)S(1)} %get-tuple-element.3211), channel_id=1, source_target_pairs={{252,0},{0,4},{4,8},{8,12},{12,16},{16,20},{20,24},{24,28},{28,32}... | collective-permute-start | bytes 393224 | tf_op jit(solution)/shard_map/while/body/eval_jaxpr/ppermute | solution.py:30
  590.5 16.7 %collective-permute-start.12 = (bf16[128,4,128]{2,0,1:T(8,128)(2,1)}, bf16[128,4,128]{2,0,1:T(8,128)(2,1)S(1)}, u32[]{:S(2)}, u32[]{:S(2)}) collective-permute-start(bf16[128,4,128]{2,0,1:T(8,128)(2,1)} %get-tuple-element.3212), channel_id=1, source_target_pairs={{252,0},{0,4},{4,8},{8,12},{12,16},{16,20},{20,24},{24,28},{28,32}... | collective-permute-start | bytes 393224 | tf_op jit(solution)/shard_map/while/body/eval_jaxpr/ppermute | solution.py:30
  590.6 18.1 %collective-permute-start.13 = (bf16[128,4,128]{2,0,1:T(8,128)(2,1)}, bf16[128,4,128]{2,0,1:T(8,128)(2,1)S(1)}, u32[]{:S(2)}, u32[]{:S(2)}) collective-permute-start(bf16[128,4,128]{2,0,1:T(8,128)(2,1)} %get-tuple-element.3213), channel_id=1, source_target_pairs={{252,0},{0,4},{4,8},{8,12},{12,16},{16,20},{20,24},{24,28},{28,32}... | collective-permute-start | bytes 393224 | tf_op jit(solution)/shard_map/while/body/eval_jaxpr/ppermute | solution.py:30
  609.6 14.4 %collective-permute-start.11 = (bf16[128,4,128]{2,0,1:T(8,128)(2,1)S(1)}, bf16[128,4,128]{2,0,1:T(8,128)(2,1)S(1)}, u32[]{:S(2)}, u32[]{:S(2)}) collective-permute-start(bf16[128,4,128]{2,0,1:T(8,128)(2,1)S(1)} %get-tuple-element.3211), channel_id=1, source_target_pairs={{252,0},{0,4},{4,8},{8,12},{12,16},{16,20},{20,24},{24,28},{28,32}... | collective-permute-start | bytes 393224 | tf_op jit(solution)/shard_map/while/body/eval_jaxpr/ppermute | solution.py:30
  609.6 15.9 %collective-permute-start.12 = (bf16[128,4,128]{2,0,1:T(8,128)(2,1)}, bf16[128,4,128]{2,0,1:T(8,128)(2,1)S(1)}, u32[]{:S(2)}, u32[]{:S(2)}) collective-permute-start(bf16[128,4,128]{2,0,1:T(8,128)(2,1)} %get-tuple-element.3212), channel_id=1, source_target_pairs={{252,0},{0,4},{4,8},{8,12},{12,16},{16,20},{20,24},{24,28},{28,32}... | collective-permute-start | bytes 393224 | tf_op jit(solution)/shard_map/while/body/eval_jaxpr/ppermute | solution.py:30
  609.6 17.2 %collective-permute-start.13 = (bf16[128,4,128]{2,0,1:T(8,128)(2,1)}, bf16[128,4,128]{2,0,1:T(8,128)(2,1)S(1)}, u32[]{:S(2)}, u32[]{:S(2)}) collective-permute-start(bf16[128,4,128]{2,0,1:T(8,128)(2,1)} %get-tuple-element.3213), channel_id=1, source_target_pairs={{252,0},{0,4},{4,8},{8,12},{12,16},{16,20},{20,24},{24,28},{28,32}... | collective-permute-start | bytes 393224 | tf_op jit(solution)/shard_map/while/body/eval_jaxpr/ppermute | solution.py:30
  627.7 13.8 %collective-permute-start.12 = (bf16[128,4,128]{2,0,1:T(8,128)(2,1)}, bf16[128,4,128]{2,0,1:T(8,128)(2,1)S(1)}, u32[]{:S(2)}, u32[]{:S(2)}) collective-permute-start(bf16[128,4,128]{2,0,1:T(8,128)(2,1)} %get-tuple-element.3212), channel_id=1, source_target_pairs={{252,0},{0,4},{4,8},{8,12},{12,16},{16,20},{20,24},{24,28},{28,32}... | collective-permute-start | bytes 393224 | tf_op jit(solution)/shard_map/while/body/eval_jaxpr/ppermute | solution.py:30
  627.7 15.1 %collective-permute-start.13 = (bf16[128,4,128]{2,0,1:T(8,128)(2,1)}, bf16[128,4,128]{2,0,1:T(8,128)(2,1)S(1)}, u32[]{:S(2)}, u32[]{:S(2)}) collective-permute-start(bf16[128,4,128]{2,0,1:T(8,128)(2,1)} %get-tuple-element.3213), channel_id=1, source_target_pairs={{252,0},{0,4},{4,8},{8,12},{12,16},{16,20},{20,24},{24,28},{28,32}... | collective-permute-start | bytes 393224 | tf_op jit(solution)/shard_map/while/body/eval_jaxpr/ppermute | solution.py:30
  643.7 15.8 %collective-permute-start.12 = (bf16[128,4,128]{2,0,1:T(8,128)(2,1)}, bf16[128,4,128]{2,0,1:T(8,128)(2,1)S(1)}, u32[]{:S(2)}, u32[]{:S(2)}) collective-permute-start(bf16[128,4,128]{2,0,1:T(8,128)(2,1)} %get-tuple-element.3212), channel_id=1, source_target_pairs={{252,0},{0,4},{4,8},{8,12},{12,16},{16,20},{20,24},{24,28},{28,32}... | collective-permute-start | bytes 393224 | tf_op jit(solution)/shard_map/while/body/eval_jaxpr/ppermute | solution.py:30
  643.7 17.9 %collective-permute-start.13 = (bf16[128,4,128]{2,0,1:T(8,128)(2,1)}, bf16[128,4,128]{2,0,1:T(8,128)(2,1)S(1)}, u32[]{:S(2)}, u32[]{:S(2)}) collective-permute-start(bf16[128,4,128]{2,0,1:T(8,128)(2,1)} %get-tuple-element.3213), channel_id=1, source_target_pairs={{252,0},{0,4},{4,8},{8,12},{12,16},{16,20},{20,24},{24,28},{28,32}... | collective-permute-start | bytes 393224 | tf_op jit(solution)/shard_map/while/body/eval_jaxpr/ppermute | solution.py:30
  750.6 13.6 %collective-permute-start.16 = (bf16[64,4,128]{2,0,1:T(8,128)(2,1)S(1)}, bf16[64,4,128]{2,0,1:T(8,128)(2,1)S(1)}, u32[]{:S(2)}, u32[]{:S(2)}) collective-permute-start(bf16[64,4,128]{2,0,1:T(8,128)(2,1)S(1)} %get-tuple-element.3104), channel_id=1, source_target_pairs={{252,0},{0,4},{4,8},{8,12},{12,16},{16,20},{20,24},{24,28},{28,32}... | collective-permute-start | bytes 196616 | tf_op jit(solution)/shard_map/while/body/eval_jaxpr/ppermute | solution.py:30
  764.6 13.4 %collective-permute-start.17 = (bf16[64,4,128]{2,0,1:T(8,128)(2,1)S(1)}, bf16[64,4,128]{2,0,1:T(8,128)(2,1)S(1)}, u32[]{:S(2)}, u32[]{:S(2)}) collective-permute-start(bf16[64,4,128]{2,0,1:T(8,128)(2,1)S(1)} %get-tuple-element.3105), channel_id=1, source_target_pairs={{252,0},{0,4},{4,8},{8,12},{12,16},{16,20},{20,24},{24,28},{28,32}... | collective-permute-start | bytes 196616 | tf_op jit(solution)/shard_map/while/body/eval_jaxpr/ppermute | solution.py:30
  764.7 14.7 %collective-permute-start.16 = (bf16[64,4,128]{2,0,1:T(8,128)(2,1)S(1)}, bf16[64,4,128]{2,0,1:T(8,128)(2,1)S(1)}, u32[]{:S(2)}, u32[]{:S(2)}) collective-permute-start(bf16[64,4,128]{2,0,1:T(8,128)(2,1)S(1)} %get-tuple-element.3104), channel_id=1, source_target_pairs={{252,0},{0,4},{4,8},{8,12},{12,16},{16,20},{20,24},{24,28},{28,32}... | collective-permute-start | bytes 196616 | tf_op jit(solution)/shard_map/while/body/eval_jaxpr/ppermute | solution.py:30
  779.8 13.2 %collective-permute-start.17 = (bf16[64,4,128]{2,0,1:T(8,128)(2,1)S(1)}, bf16[64,4,128]{2,0,1:T(8,128)(2,1)S(1)}, u32[]{:S(2)}, u32[]{:S(2)}) collective-permute-start(bf16[64,4,128]{2,0,1:T(8,128)(2,1)S(1)} %get-tuple-element.3105), channel_id=1, source_target_pairs={{252,0},{0,4},{4,8},{8,12},{12,16},{16,20},{20,24},{24,28},{28,32}... | collective-permute-start | bytes 196616 | tf_op jit(solution)/shard_map/while/body/eval_jaxpr/ppermute | solution.py:30
  779.9 13.8 %collective-permute-start.16 = (bf16[64,4,128]{2,0,1:T(8,128)(2,1)S(1)}, bf16[64,4,128]{2,0,1:T(8,128)(2,1)S(1)}, u32[]{:S(2)}, u32[]{:S(2)}) collective-permute-start(bf16[64,4,128]{2,0,1:T(8,128)(2,1)S(1)} %get-tuple-element.3104), channel_id=1, source_target_pairs={{252,0},{0,4},{4,8},{8,12},{12,16},{16,20},{20,24},{24,28},{28,32}... | collective-permute-start | bytes 196616 | tf_op jit(solution)/shard_map/while/body/eval_jaxpr/ppermute | solution.py:30
  794.3 13.1 %collective-permute-start.16 = (bf16[64,4,128]{2,0,1:T(8,128)(2,1)S(1)}, bf16[64,4,128]{2,0,1:T(8,128)(2,1)S(1)}, u32[]{:S(2)}, u32[]{:S(2)}) collective-permute-start(bf16[64,4,128]{2,0,1:T(8,128)(2,1)S(1)} %get-tuple-element.3104), channel_id=1, source_target_pairs={{252,0},{0,4},{4,8},{8,12},{12,16},{16,20},{20,24},{24,28},{28,32}... | collective-permute-start | bytes 196616 | tf_op jit(solution)/shard_map/while/body/eval_jaxpr/ppermute | solution.py:30
  857.4 20.6 %collective-permute-start.21 = (bf16[256,4,128]{0,2,1:T(8,128)(2,1)S(1)}, bf16[256,4,128]{0,2,1:T(8,128)(2,1)}, u32[]{:S(2)}, u32[]{:S(2)}) collective-permute-start(bf16[256,4,128]{0,2,1:T(8,128)(2,1)S(1)} %copy.538), channel_id=1, source_target_pairs={{12,0},{16,4},{20,8},{24,12},{28,16},{32,20},{36,24},{40,28},{44,3... | collective-permute-start | bytes 786440 | tf_op jit(solution)/shard_map/ppermute | solution.py:30
  860.3 16.7 %collective-permute-start.22 = (bf16[128,4,128]{2,0,1:T(8,128)(2,1)S(1)}, bf16[128,4,128]{2,0,1:T(8,128)(2,1)S(1)}, u32[]{:S(2)}, u32[]{:S(2)}) collective-permute-start(bf16[128,4,128]{2,0,1:T(8,128)(2,1)S(1)} %copy-done.47), channel_id=1, source_target_pairs={{28,0},{32,4},{36,8},{40,12},{44,16},{48,20},{52,24},{56,28},{60,3... | collective-permute-start | bytes 393224 | tf_op jit(solution)/shard_map/ppermute | solution.py:30
  860.3 16.8 %collective-permute-start.19 = (bf16[128,4,128]{2,0,1:T(8,128)(2,1)S(1)}, bf16[128,4,128]{2,0,1:T(8,128)(2,1)S(1)}, u32[]{:S(2)}, u32[]{:S(2)}) collective-permute-start(bf16[128,4,128]{2,0,1:T(8,128)(2,1)S(1)} %copy-done.48), channel_id=1, source_target_pairs={{28,0},{32,4},{36,8},{40,12},{44,16},{48,20},{52,24},{56,28},{60,3... | collective-permute-start | bytes 393224 | tf_op jit(solution)/shard_map/ppermute | solution.py:30
  (217 other events, 5990.3 us)
